TPU v7x, 128 devices: a whole 4x4x4 slice. The times are simulated.
128 devices in a mesh: zone: 8 (over x, core), row: 16 (over y, z).
Axes of the slice: x: 4, y: 4, z: 4, core: 2. Of those that a mesh axis runs over, the one named last changes fastest.
Arguments:
- block_input: bfloat16 [512, 256, 1024], P('row', 'zone'), may hold values from -6 to 6
- cotangent: bfloat16 [512, 256, 1024], P('row', 'zone'), may hold values from -6 to 6
- w_up: bfloat16 [1024, 2048], replicated, may hold values from -0.1875 to 0.1875
- w_down: bfloat16 [2048, 1024], replicated, may hold values from -0.125 to 0.125
- ln_gain: float32 [1024], replicated, may hold values from 0.5 to 1.5
- pair_live: int32 [16, 8, 3], P('row', 'zone'), may hold values 0 or 1
- row_interp: bfloat16 [16, 8, 3, 32, 48], P('row', 'zone'), may hold values from -1 to 1
- col_interp: bfloat16 [16, 8, 3, 32, 48], P('row', 'zone'), may hold values from -1 to 1
Outputs:
- source_grad: bfloat16 [768, 384, 1024], P('row', 'zone')
- up_grad: float32 [1024, 2048], P(('zone', 'row'))
- down_grad: float32 [2048, 1024], P(('zone', 'row'))
- gain_grad: float32 [1024], P(('zone', 'row'))
All inputs are finite; a program needn't handle non-finite values. No bound on the sum of `pair_live` on one device may be relied on, other than what follows from the above.
Results may differ from a plain program's by a relative error of at most 0.02.
Values may be sent and summed in bfloat16 or wider, within the bound.
A program may use at most 128 MiB of HBM per device.

v0:
```python
import math

import jax
import jax.numpy as jnp
from jax import lax
from jax.sharding import PartitionSpec as P

ROOT_HALF = 0.7071067811865476
INV_ROOT_TAU = 0.3989422804014327
epsilon = 1e-05


def cut_along(array, dim, length):
    before, after = (array.shape[:dim], array.shape[dim + 1 :])
    return jnp.moveaxis(array.reshape(*before, length, -1, *after), dim, 0)


def sum_packed(arrays, axis, dims):
    length = lax.axis_size(axis)
    parts = [cut_along(a, dim, length) for a, dim in zip(arrays, dims)]
    lines = jnp.concatenate([b.reshape(length, -1) for b in parts], axis=1)
    width = max(16, -(-lines.shape[1] // 1024) * 8)
    lines = jnp.pad(lines, ((0, 0), (0, width * 128 - lines.shape[1]))).reshape(-1, 128)
    ravelled, at, outs = (lax.psum_scatter(lines, axis, tiled=True).reshape(-1), 0, [])
    for b in parts:
        part = b[0]
        outs.append(ravelled[at : at + part.size].reshape(part.shape))
        at += part.size
    return tuple(outs)


def shifted_2(value, axis, steps):
    count = lax.axis_size(axis)
    initial, last = (max(0, -steps), min(count, count - steps))
    return lax.ppermute(value, axis, [(source, source + steps) for source in range(initial, last)])


def gelu_value(pre):
    return pre * 0.5 * (1.0 + lax.erf(pre * ROOT_HALF))


def gelu_slope(pre):
    return 0.5 * (1.0 + lax.erf(pre * ROOT_HALF)) + pre * jnp.exp(-0.5 * pre * pre) * INV_ROOT_TAU


def pull_back(grid_block, rows_live, cols):
    half = jnp.einsum("ijc,jl->ilc", grid_block, cols, preferred_element_type=jnp.float32).astype(
        jnp.bfloat16
    )
    return jnp.einsum("im,ilc->mlc", rows_live, half, preferred_element_type=jnp.float32).astype(
        jnp.bfloat16
    )


def on_device(block_input, cotangent, w_up, w_down, ln_gain, pair_live, row_interp, col_interp):
    side = block_input.shape[0]
    width = block_input.shape[2]
    inputs = block_input.reshape(side * side, width)
    upstream = cotangent.reshape(side * side, width)
    values = inputs.astype(jnp.float32)
    center = jnp.mean(values, -1, keepdims=True)
    shifted = values - center
    spread = jnp.mean(shifted * shifted, -1, keepdims=True)
    inv_std = lax.rsqrt(spread + epsilon)
    normal = shifted * inv_std
    normed = (normal * ln_gain).astype(jnp.bfloat16)
    pre = jnp.dot(normed, w_up, preferred_element_type=jnp.float32)
    activated = gelu_value(pre).astype(jnp.bfloat16)
    back_act = jnp.dot(upstream, w_down.T, preferred_element_type=jnp.float32)
    back_pre = (back_act * gelu_slope(pre)).astype(jnp.bfloat16)
    factor = 1.0 / math.sqrt(side * side * lax.axis_size("zone") * lax.axis_size("row"))
    down_term = jnp.dot(activated.T, upstream, preferred_element_type=jnp.float32) * factor
    up_term = jnp.dot(normed.T, back_pre, preferred_element_type=jnp.float32) * factor
    back_norm = jnp.dot(back_pre, w_up.T, preferred_element_type=jnp.float32)
    gain_term = jnp.sum(back_norm * normal, 0) * factor
    scaled = back_norm * ln_gain
    grad_in = upstream.astype(jnp.float32) + inv_std * (
        scaled
        - jnp.mean(scaled, -1, keepdims=True)
        - normal * jnp.mean(scaled * normal, -1, keepdims=True)
    )
    grid_block = grad_in.astype(jnp.bfloat16).reshape(side, side, width)
    partial_sums = (
        lax.psum_scatter(
            up_term.astype(jnp.bfloat16), "zone", scatter_dimension=0, tiled=True
        ).astype(jnp.float32),
        lax.psum_scatter(
            down_term.astype(jnp.bfloat16), "zone", scatter_dimension=0, tiled=True
        ).astype(jnp.float32),
        lax.psum_scatter(
            gain_term.astype(jnp.bfloat16), "zone", scatter_dimension=0, tiled=True
        ).astype(jnp.float32),
    )
    up_grad, down_grad, gain_grad = tuple(
        (
            part.astype(jnp.float32)
            for part in sum_packed(
                (
                    partial_sums[0].astype(jnp.bfloat16),
                    partial_sums[1].astype(jnp.bfloat16),
                    partial_sums[2].astype(jnp.bfloat16),
                ),
                "row",
                (0, 0, 0),
            )
        )
    )
    live_rows = [
        row_interp[0, 0, slot] * pair_live[0, 0, slot].astype(jnp.bfloat16) for slot in range(3)
    ]
    own_piece = pull_back(grid_block, live_rows[1], col_interp[0, 0, 1])
    above_block, above_rows, above_cols = shifted_2(
        (grid_block, live_rows[0], col_interp[0, 0, 0]), "row", -1
    )
    below_block, below_rows, below_cols = shifted_2(
        (grid_block, live_rows[2], col_interp[0, 0, 2]), "row", 1
    )
    from_above = pull_back(above_block, above_rows, above_cols)
    from_below = pull_back(below_block, below_rows, below_cols)
    total = (
        own_piece.astype(jnp.float32)
        + from_above.astype(jnp.float32)
        + from_below.astype(jnp.float32)
    )
    return (total.astype(jnp.bfloat16), up_grad, down_grad, gain_grad)


def solution(mesh):
    in_specs = (
        P("row", "zone", None),
        P("row", "zone", None),
        P(),
        P(),
        P(),
        P("row", "zone", None),
        P("row", "zone", None, None, None),
        P("row", "zone", None, None, None),
    )
    out_specs = (
        P("row", "zone", None),
        P(("zone", "row"), None),
        P(("zone", "row"), None),
        P(("zone", "row")),
    )
    return jax.shard_map(
        on_device, mesh=mesh, in_specs=in_specs, out_specs=out_specs, check_vma=False
    )
```

profile of v0, /device:TPU:0, one launch (start us, length us, event | category | flops | bytes accessed | tf_op | source)
XLA Modules:
  0.0 231.8 jit_solution(11491905136705918213)
XLA Ops:
  7.2 0.0 copy-start
  7.2 0.0 reduce-scatter.5.cloned.1.call-start
  7.2 2.1 convert_reduce_fusion
  9.3 0.1 div.16
  9.4 2.3 multiply_reduce_fusion.2
  11.7 0.1 rsqrt.12
  11.8 0.0 copy-start.8
  11.8 0.7 multiply_convert_fusion.4
  12.5 1.5 copy-done.8
  14.0 4.5 %fusion.33 = f32[1024,2048]{1,0:T(8,128)S(1)} fusion(bf16[1024,1024]{1,0:T(8,128)(2,1)S(1)} %multiply_convert_fusion.4, bf16[1024,2048]{1,0:T(8,128)(2,1)S(1)} %copy-done.8), kind=kOutput, calls=%fused_computation.62 | convolution fusion | flops 4294967296 | bytes 14680064 | tf_op jit(solution)/shard_map/dot_general | solution.py:67
  18.5 3.2 %copy-done.13 = f32[1024,2048]{1,0:T(8,128)} copy-done((f32[1024,2048]{1,0:T(8,128)}, f32[1024,2048]{1,0:T(8,128)S(1)}, u32[]{:S(2)}) %copy-start.13) | copy-done | bytes 8388632
  21.8 6.3 %multiply_convert_fusion = bf16[2048,1024]{1,0:T(8,128)(2,1)} fusion(bf16[1024,1024]{1,0:T(8,128)(2,1)S(1)} %bitcast.71, f32[1024,2048]{1,0:T(8,128)S(1)} %fusion.33), kind=kOutput, calls=%fused_computation.8 | convolution fusion | flops 4309647360 | bytes 14680064 | tf_op jit(solution)/shard_map/dot_general | solution.py:72
  28.0 0.0 reduce-scatter.5.cloned.1.call-update
  28.1 0.0 reduce-scatter.3.cloned.1.call-start
  28.1 10.3 %fusion.5 = bf16[1024,2048]{1,0:T(8,128)(2,1)S(1)} fusion(f32[1024,2048]{1,0:T(8,128)} %copy-done.13, bf16[1024,1024]{1,0:T(8,128)(2,1)} %bitcast.70, bf16[2048,1024]{1,0:T(8,128)(2,1)} %param.11), kind=kOutput, calls=%fused_computation.7 | convolution fusion | flops 4315938816 | bytes 18874368 | tf_op jit(solution)/shard_map/dot_general | solution.py:69
  38.4 0.0 copy-start.12
  38.4 2.0 copy-done.12
  40.4 6.3 %multiply_convert_fusion.2 = bf16[1024,2048]{1,0:T(8,128)(2,1)} fusion(bf16[1024,1024]{1,0:T(8,128)(2,1)S(1)} %copy-done.4, bf16[1024,2048]{1,0:T(8,128)(2,1)S(1)} %fusion.5), kind=kOutput, calls=%fused_computation.10 | convolution fusion | flops 4299161600 | bytes 10485760 | tf_op jit(solution)/shard_map/dot_general | solution.py:73
  46.7 0.0 reduce-scatter.3.cloned.1.call-update
  46.7 0.2 all-reduce.5.cloned.1.call-start
  47.0 0.0 copy-start.2
  47.0 8.7 %multiply_reduce_fusion = (f32[1024]{0:T(1024)S(1)}, f32[1024]{0:T(1024)S(1)}, f32[1024]{0:T(1024)S(1)}, f32[1024,1024]{1,0:T(8,128)S(1)}) fusion(bf16[32,32,1024]{2,1,0:T(8,128)(2,1)S(1)} %copy-done, f32[1024]{0:T(1024)S(1)} %div.16, f32[1024]{0:T(1024)S(1)} %rsqrt.12, f32[1024]{0:T(1024)S(1)} %copy-done.7, bf16[1024,2048]{1,0:T(8,128)(2,1)} %copy-done.12, ...), kind=kOutput, calls=%fused_computation.14 | convolution fusion | flops 4304401408 | bytes 14704640 | tf_op jit(solution)/shard_map/dot_general | solution.py:74
  55.7 0.0 copy-start.5
  55.7 0.0 copy-start.9
  55.7 0.0 copy-start.6
  55.7 3.0 %add_convert_fusion.1 = bf16[1024,1024]{1,0:T(8,128)(2,1)} fusion(f32[1024,1024]{1,0:T(8,128)S(1)} %get-tuple-element.28, bf16[32,32,1024]{2,1,0:T(8,128)(2,1)S(1)} %copy-done, f32[1024]{0:T(1024)S(1)} %get-tuple-element.29, f32[1024]{0:T(1024)S(1)} %get-tuple-element.30, f32[1024]{0:T(1024)S(1)} %copy-done.7, f32[1024]{0:T(1024)S(1)} %div.16, ...), kind=kLoop, calls=%fused_computation.15 | loop fusion | flops 11534336 | bytes 10506240 | tf_op jit(solution)/shard_map/convert_element_type | solution.py:82
  58.8 1.3 collective-permute-start.1
  60.0 4.7 %collective-permute-start.4 = (bf16[32,32,1024]{2,1,0:T(8,128)(2,1)}, bf16[32,32,1024]{2,1,0:T(8,128)(2,1)S(1)}, u32[]{:S(2)}, u32[]{:S(2)}) collective-permute-start(bf16[32,32,1024]{2,1,0:T(8,128)(2,1)} %bitcast.5), channel_id=1, source_target_pairs={{0,1},{1,2},{2,3},{3,4},{4,5},{5,6},{6,7},{7,8},{8,9},{9,10},{10,1... | collective-permute-start | bytes 6291464 | tf_op jit(solution)/shard_map/ppermute | solution.py:35
  64.8 3.8 %collective-permute-start.5 = (bf16[32,48]{1,0:T(8,128)(2,1)S(1)}, bf16[32,48]{1,0:T(8,128)(2,1)S(1)}, u32[]{:S(2)}, u32[]{:S(2)}) collective-permute-start(bf16[32,48]{1,0:T(8,128)(2,1)S(1)} %get-tuple-element.23), channel_id=1, source_target_pairs={{0,1},{1,2},{2,3},{3,4},{4,5},{5,6},{6,7},{7,8},{8,9},{9,10},{10,1... | collective-permute-start | bytes 9224 | tf_op jit(solution)/shard_map/ppermute | solution.py:35
  68.6 1.3 collective-permute-start.2
  69.9 0.6 fusion.32
  70.5 1.3 multiply_bitcast_fusion
  71.8 4.5 %collective-permute-start.3 = (bf16[32,48]{1,0:T(8,128)(2,1)S(1)}, bf16[32,48]{1,0:T(8,128)(2,1)S(1)}, u32[]{:S(2)}, u32[]{:S(2)}) collective-permute-start(bf16[32,48]{1,0:T(8,128)(2,1)S(1)} %get-tuple-element.21), channel_id=1, source_target_pairs={{0,1},{1,2},{2,3},{3,4},{4,5},{5,6},{6,7},{7,8},{8,9},{9,10},{10,1... | collective-permute-start | bytes 9224 | tf_op jit(solution)/shard_map/ppermute | solution.py:35
  76.3 2.7 %convert_bitcast_fusion.2 = bf16[32,48,1024]{2,1,0:T(8,128)(2,1)S(1)} fusion(bf16[32,32,1024]{2,1,0:T(8,128)(2,1)} %bitcast.5, bf16[1,1,3,32,48]{4,3,2,1,0:T(8,128)(2,1)S(1)} %copy-done.5), kind=kOutput, calls=%fused_computation.29 | convolution fusion | flops 102236160 | bytes 5251072 | tf_op jit(solution)/shard_map/ijc,jl->ilc/dot_general | solution.py:47
  79.0 0.0 copy-start.11
  79.0 0.0 copy-start.10
  79.0 7.6 %fusion.14 = bf16[48,48,1024]{2,0,1:T(8,128)(2,1)} fusion(bf16[32,48,1024]{2,1,0:T(8,128)(2,1)S(1)} %convert_bitcast_fusion.2, bf16[1,1,3,32,48]{4,3,2,1,0:T(8,128)(2,1)S(1)} %copy-done.6, bf16[]{:T(256)} %bitcast), kind=kOutput, calls=%fused_computation.25 | convolution fusion | flops 151001088 | bytes 7872514 | tf_op jit(solution)/shard_map/im,ilc->mlc/dot_general | solution.py:50
  86.6 0.6 dynamic-slice.2
  87.2 0.6 dynamic-slice
  88.5 13.5 %all-reduce.1 = bf16[1024]{0:T(1024)(128)(2,1)S(1)} all-reduce(bf16[1024]{0:T(1024)(128)(2,1)S(1)} %multiply_convert_fusion.5), channel_id=4, replica_groups=mesh['zone'=8,'row'=16] {'zone'}, use_global_device_ids=true, to_apply=%region_7.0.clone | all-reduce | flops 1024 | bytes 4096
  102.0 0.1 dynamic-slice.1
  102.1 0.1 reshape.88
  102.8 5.8 %collective-permute-done.2 = bf16[32,48]{1,0:T(8,128)(2,1)S(1)} collective-permute-done((bf16[32,48]{1,0:T(8,128)(2,1)S(1)}, bf16[32,48]{1,0:T(8,128)(2,1)S(1)}, u32[]{:S(2)}, u32[]{:S(2)}) %collective-permute-start.2) | collective-permute-done | bytes 3104 | tf_op jit(solution)/shard_map/ppermute | solution.py:35
  108.7 1.3 collective-permute-start
  109.9 0.0 collective-permute-done.1
  110.0 2.7 %convert_bitcast_fusion.1 = bf16[32,48,1024]{2,1,0:T(8,128)(2,1)S(1)} fusion(bf16[32,32,1024]{2,1,0:T(8,128)(2,1)} %collective-permute-done.1, bf16[32,48]{1,0:T(8,128)(2,1)S(1)} %collective-permute-done.2), kind=kOutput, calls=%fused_computation.28 | convolution fusion | flops 102236160 | bytes 5245952 | tf_op jit(solution)/shard_map/ijc,jl->ilc/dot_general | solution.py:47
  112.6 1.6 collective-permute-done
  114.2 7.0 %fusion.12 = bf16[48,48,1024]{2,0,1:T(8,128)(2,1)} fusion(bf16[32,48,1024]{2,1,0:T(8,128)(2,1)S(1)} %convert_bitcast_fusion.1, bf16[32,48]{1,0:T(8,128)(2,1)S(1)} %collective-permute-done), kind=kOutput, calls=%fused_computation.23 | convolution fusion | flops 150994944 | bytes 7867392 | tf_op jit(solution)/shard_map/im,ilc->mlc/dot_general | solution.py:50
  121.2 2.1 reshape_reshape.7
  123.3 2.1 reshape_reshape.6
  125.4 1.3 fusion.20
  126.6 1.6 reshape.89
  128.2 0.0 all-reduce.5.cloned.1.call-update
  128.2 0.0 collective-permute-done.5
  128.2 0.0 collective-permute-done.4
  128.3 1.1 convert_bitcast_fusion
  129.4 8.9 %add_convert_fusion = bf16[48,48,1024]{2,0,1:T(8,128)(2,1)S(1)} fusion(bf16[48,48,1024]{2,0,1:T(8,128)(2,1)} %fusion.12, bf16[48,48,1024]{2,0,1:T(8,128)(2,1)} %fusion.14, bf16[32,48,1024]{2,1,0:T(8,128)(2,1)S(1)} %convert_bitcast_fusion, bf16[32,48]{1,0:T(8,128)(2,1)S(1)} %collective-permute-done.3), kind=kOutput, calls=%fused_computation.1 | convolution fusion | flops 167510016 | bytes 17304576 | tf_op jit(solution)/shard_map/im,ilc->mlc/dot_general | solution.py:50
  138.3 4.8 %copy.17 = bf16[48,48,1024]{2,1,0:T(8,128)(2,1)} copy(bf16[48,48,1024]{2,0,1:T(8,128)(2,1)S(1)} %add_convert_fusion) | data formatting | bytes 9437184
  143.1 78.7 %all-reduce.5.cloned.1.call-done = bf16[4224,128]{1,0:T(8,128)(2,1)} async-done(((bf16[4224,128]{1,0:T(8,128)(2,1)}), bf16[4224,128]{1,0:T(8,128)(2,1)}) %all-reduce.5.cloned.1.call-update) | async-done | bytes 1081360
  221.8 0.9 dynamic-slice_bitcast_fusion
  222.7 0.5 slice_convert_fusion
  223.2 0.8 dynamic-slice_convert_fusion
  224.0 0.6 reshape.93
  224.7 0.6 reshape.92
  (25 shorter events, 0.1 us)
Async XLA Ops:
  7.2 4.6 %copy-start = (bf16[32,32,1024]{2,1,0:T(8,128)(2,1)S(1)}, bf16[32,32,1024]{2,1,0:T(8,128)(2,1)}, u32[]{:S(2)}) copy-start(bf16[32,32,1024]{2,1,0:T(8,128)(2,1)} %param.8) | copy-start | bytes 6291460
  7.2 4.6 %copy-start.7 = (f32[1024]{0:T(1024)S(1)}, f32[1024]{0:T(1024)}, u32[]{:S(2)}) copy-start(f32[1024]{0:T(1024)} %param.12) | copy-start | bytes 12292
  7.2 114.0 %reduce-scatter.5.cloned.1.call-start = ((), (), s32[]{:S(2)}) async-start(), calls=%async_computation.3 | async-start | bytes 4718592 | tf_op jit(solution)/shard_map/reduce_scatter | solution.py:87
  11.8 2.2 copy-start.8
  14.0 4.5 %copy-start.3 = (bf16[1024,1024]{1,0:T(8,128)(2,1)}, bf16[1024,1024]{1,0:T(8,128)(2,1)S(1)}, u32[]{:S(2)}) copy-start(bf16[1024,1024]{1,0:T(8,128)(2,1)S(1)} %multiply_convert_fusion.4) | copy-start | bytes 6291460
  14.0 7.8 %copy-start.1 = (bf16[32,32,1024]{2,1,0:T(8,128)(2,1)S(1)}, bf16[32,32,1024]{2,1,0:T(8,128)(2,1)}, u32[]{:S(2)}) copy-start(bf16[32,32,1024]{2,1,0:T(8,128)(2,1)} %param.9) | copy-start | bytes 6291460
  18.5 3.2 %copy-start.13 = (f32[1024,2048]{1,0:T(8,128)}, f32[1024,2048]{1,0:T(8,128)S(1)}, u32[]{:S(2)}) copy-start(f32[1024,2048]{1,0:T(8,128)S(1)} %fusion.33) | copy-start | bytes 25165828
  28.1 95.2 %reduce-scatter.3.cloned.1.call-start = ((), (), s32[]{:S(2)}) async-start(), calls=%async_computation.2 | async-start | bytes 4718592 | tf_op jit(solution)/shard_map/reduce_scatter | solution.py:84
  28.1 12.3 %copy-start.4 = (bf16[1024,1024]{1,0:T(8,128)(2,1)S(1)}, bf16[1024,1024]{1,0:T(8,128)(2,1)}, u32[]{:S(2)}) copy-start(bf16[1024,1024]{1,0:T(8,128)(2,1)} %copy-done.3) | copy-start | bytes 6291460
  38.4 2.0 copy-start.12
  46.7 175.1 %all-reduce.5.cloned.1.call-start = ((), (), s32[]{:S(2)}) async-start(), calls=%async_computation.4 | async-start | bytes 2162688
  47.0 8.7 %copy-start.2 = (bf16[32,32,1024]{2,1,0:T(8,128)(2,1)S(1)}, bf16[32,32,1024]{2,1,0:T(8,128)(2,1)}, u32[]{:S(2)}) copy-start(bf16[32,32,1024]{2,1,0:T(8,128)(2,1)} %param.9) | copy-start | bytes 6291460
  55.7 9.0 %copy-start.5 = (bf16[1,1,3,32,48]{4,3,2,1,0:T(8,128)(2,1)S(1)}, bf16[1,1,3,32,48]{4,3,2,1,0:T(8,128)(2,1)}, u32[]{:S(2)}) copy-start(bf16[1,1,3,32,48]{4,3,2,1,0:T(8,128)(2,1)} %param.15) | copy-start | bytes 27652
  55.7 14.2 %copy-start.9 = (s32[1,1,3]{2,1,0:T(1,128)S(1)}, s32[1,1,3]{2,1,0:T(1,128)}, u32[]{:S(2)}) copy-start(s32[1,1,3]{2,1,0:T(1,128)} %param.13) | copy-start | bytes 40
  55.7 14.7 %copy-start.6 = (bf16[1,1,3,32,48]{4,3,2,1,0:T(8,128)(2,1)S(1)}, bf16[1,1,3,32,48]{4,3,2,1,0:T(8,128)(2,1)}, u32[]{:S(2)}) copy-start(bf16[1,1,3,32,48]{4,3,2,1,0:T(8,128)(2,1)} %param.14) | copy-start | bytes 27652
  58.8 51.2 %collective-permute-start.1 = (bf16[32,32,1024]{2,1,0:T(8,128)(2,1)}, bf16[32,32,1024]{2,1,0:T(8,128)(2,1)}, u32[]{:S(2)}, u32[]{:S(2)}) collective-permute-start(bf16[32,32,1024]{2,1,0:T(8,128)(2,1)} %bitcast.5), channel_id=1, source_target_pairs={{1,0},{2,1},{3,2},{4,3},{5,4},{6,5},{7,6},{8,7},{9,8},{10,9},{11,1... | collective-permute-start | bytes 6291464 | tf_op jit(solution)/shard_map/ppermute | solution.py:35
  60.0 68.2 %collective-permute-start.4 = (bf16[32,32,1024]{2,1,0:T(8,128)(2,1)}, bf16[32,32,1024]{2,1,0:T(8,128)(2,1)S(1)}, u32[]{:S(2)}, u32[]{:S(2)}) collective-permute-start(bf16[32,32,1024]{2,1,0:T(8,128)(2,1)} %bitcast.5), channel_id=1, source_target_pairs={{0,1},{1,2},{2,3},{3,4},{4,5},{5,6},{6,7},{7,8},{8,9},{9,10},{10,1... | collective-permute-start | bytes 6291464 | tf_op jit(solution)/shard_map/ppermute | solution.py:35
  64.8 63.5 %collective-permute-start.5 = (bf16[32,48]{1,0:T(8,128)(2,1)S(1)}, bf16[32,48]{1,0:T(8,128)(2,1)S(1)}, u32[]{:S(2)}, u32[]{:S(2)}) collective-permute-start(bf16[32,48]{1,0:T(8,128)(2,1)S(1)} %get-tuple-element.23), channel_id=1, source_target_pairs={{0,1},{1,2},{2,3},{3,4},{4,5},{5,6},{6,7},{7,8},{8,9},{9,10},{10,1... | collective-permute-start | bytes 9224 | tf_op jit(solution)/shard_map/ppermute | solution.py:35
  68.6 40.1 %collective-permute-start.2 = (bf16[32,48]{1,0:T(8,128)(2,1)S(1)}, bf16[32,48]{1,0:T(8,128)(2,1)S(1)}, u32[]{:S(2)}, u32[]{:S(2)}) collective-permute-start(bf16[32,48]{1,0:T(8,128)(2,1)S(1)} %get-tuple-element.24), channel_id=1, source_target_pairs={{1,0},{2,1},{3,2},{4,3},{5,4},{6,5},{7,6},{8,7},{9,8},{10,9},{11,1... | collective-permute-start | bytes 9224 | tf_op jit(solution)/shard_map/ppermute | solution.py:35
  71.8 57.6 %collective-permute-start.3 = (bf16[32,48]{1,0:T(8,128)(2,1)S(1)}, bf16[32,48]{1,0:T(8,128)(2,1)S(1)}, u32[]{:S(2)}, u32[]{:S(2)}) collective-permute-start(bf16[32,48]{1,0:T(8,128)(2,1)S(1)} %get-tuple-element.21), channel_id=1, source_target_pairs={{0,1},{1,2},{2,3},{3,4},{4,5},{5,6},{6,7},{7,8},{8,9},{9,10},{10,1... | collective-permute-start | bytes 9224 | tf_op jit(solution)/shard_map/ppermute | solution.py:35
  79.0 7.6 %copy-start.11 = (u32[128]{0:T(128)S(1)}, u32[128]{0:T(128)}, u32[]{:S(2)}) copy-start(u32[128]{0:T(128)} %constant.38) | copy-start | bytes 1540
  79.0 8.2 %copy-start.10 = (u32[128]{0:T(128)S(1)}, u32[128]{0:T(128)}, u32[]{:S(2)}) copy-start(u32[128]{0:T(128)} %constant.34) | copy-start | bytes 1540
  108.7 5.5 %collective-permute-start = (bf16[32,48]{1,0:T(8,128)(2,1)S(1)}, bf16[32,48]{1,0:T(8,128)(2,1)S(1)}, u32[]{:S(2)}, u32[]{:S(2)}) collective-permute-start(bf16[32,48]{1,0:T(8,128)(2,1)S(1)} %get-tuple-element.22), channel_id=1, source_target_pairs={{1,0},{2,1},{3,2},{4,3},{5,4},{6,5},{7,6},{8,7},{9,8},{10,9},{11,1... | collective-permute-start | bytes 9224 | tf_op jit(solution)/shard_map/ppermute | solution.py:35
Sparse Core Ops, SparseCore 0:
  28.2 40.4 reduce-scatter.4
  71.1 36.8 reduce-scatter.2
  128.4 93.4 all-reduce.4
where the time goes:
time: 233 us; the launch traced here: 232 us
  waiting for transfers between devices  86.2 us (37%)
  matrix products  66 us (28%)
  local copies, waits for them, and re-layouts  21.6 us (9%)
  starting transfers between devices  17.2 us (7%)
  between operations  15.4 us (7%)
  blocking collectives  13.5 us (6%)
  other arithmetic  12 us (5%)
    unnamed x4, waiting for transfers between devices  78.8 us
    dot_general x3, matrix products, pull_back(): jnp.einsum('im,ilc->mlc', rows_live, half, preferred_element_type=jnp.flo...  23.5 us
    ppermute x6, starting transfers between devices, shifted_2(): lax.ppermute(value, axis, [(source, source + steps) for source in range(i...  16.9 us
    unnamed x1, blocking collectives  13.5 us
    unnamed x32, local copies, waits for them, and re-layouts  12.8 us
    dot_general x1, matrix products, on_device(): back_act = jnp.dot(upstream, w_down.T, preferred_element_type=jnp.float32)  10.3 us
    dot_general x1, matrix products, on_device(): back_norm = jnp.dot(back_pre, w_up.T, preferred_element_type=jnp.float32)  8.68 us
    ppermute x6, waiting for transfers between devices, shifted_2(): lax.ppermute(value, axis, [(source, source + steps) for source in range(i...  7.39 us
  transfers between devices with their start and end apart: 9, of which 3 were waited for; matrix products, arithmetic and copies ran while one was open for 32% of the time, Pallas kernels for 0%

commit v1 on v0

v1 whole, which is shorter than its diff:
```python
import functools
import math

import jax
import jax.numpy as jnp
from jax import lax
from jax.experimental import pallas as pl
from jax.experimental.pallas import tpu as pltpu
from jax.sharding import PartitionSpec as P

MESH = pl.DeviceIdType.MESH
BF = jnp.bfloat16
F32 = jnp.float32
ROOT_HALF = 0.7071067811865476
INV_ROOT_TAU = 0.3989422804014327
EPS = 1e-05
D = 1024
FF = 2048
TOK = 1024
CH = 256
NCH = TOK // CH
FB = 512
N_SEM = 64


def nt(a, b):
    return lax.dot_general(a, b, (((1,), (1,)), ((), ())), preferred_element_type=F32)


def tn(a, b):
    return lax.dot_general(a, b, (((0,), (0,)), ((), ())), preferred_element_type=F32)


def nn(a, b):
    return lax.dot_general(a, b, (((1,), (0,)), ((), ())), preferred_element_type=F32)


def front(
    factor,
    live_ref,
    x_hbm,
    ct_hbm,
    wu_hbm,
    wd_hbm,
    gain_ref,
    rowi_ref,
    coli_ref,
    gg_out,
    ga_out,
    gb_out,
    mats_out,
    up_out,
    down_out,
    gain_out,
    xv,
    ct,
    wu,
    wd,
    normed,
    act,
    bp,
    gg,
    normal,
    inv_s,
    bn_s,
    grad,
    part,
    xa,
    xb,
    tt,
    ya,
    yb,
    uu,
    za,
    zb,
    mats,
    mrecv,
    gacc,
    gsrc,
    grecv,
    in_sem,
    out_sem,
    send_sem,
    recv_sem,
    halo_send,
    halo_recv,
):
    zone = lax.axis_index("zone")
    row = lax.axis_index("row")
    x = zone // 2
    c = zone - 2 * x
    y = row // 4
    z = row - 4 * y

    def mod4(v):
        return lax.rem(v, 4)

    def dx(j):
        return (2 * mod4(x + j) + c, row)

    def dy(j):
        return (zone, 4 * mod4(y + j) + z)

    def dz(j):
        return (zone, 4 * y + mod4(z + j))

    pair = (2 * x + (1 - c), row)
    upper = (zone, lax.rem(row + 1, 16))
    lower = (zone, lax.rem(row + 15, 16))

    loads = []
    for n, (src, dst) in enumerate(
        [(x_hbm.at[pl.ds(0, CH)], xv.at[pl.ds(0, CH)]), (wu_hbm, wu),
         (ct_hbm.at[pl.ds(0, CH)], ct.at[pl.ds(0, CH)]), (wd_hbm, wd),
         (x_hbm.at[pl.ds(CH, TOK - CH)], xv.at[pl.ds(CH, TOK - CH)]),
         (ct_hbm.at[pl.ds(CH, TOK - CH)], ct.at[pl.ds(CH, TOK - CH)])]
    ):
        cp = pltpu.make_async_copy(src, dst, in_sem.at[n])
        cp.start()
        loads.append(cp)

    barrier = pltpu.get_barrier_semaphore()
    peers = [pair, upper, lower] + [f(j) for f in (dx, dy, dz) for j in (1, 2, 3)]
    for peer in peers:
        pl.semaphore_signal(barrier, inc=1, device_id=peer, device_id_type=MESH)

    counter = [0]

    def remote(src, dst, device):
        k = counter[0]
        counter[0] += 1
        return pltpu.make_async_remote_copy(
            src_ref=src, dst_ref=dst, send_sem=send_sem.at[k], recv_sem=recv_sem.at[k],
            device_id=device, device_id_type=MESH,
        )

    mats[...] = jnp.zeros_like(mats)
    for k in range(3):
        keep = live_ref[0, k]
        if k == 0:
            keep = jnp.where(row > 0, keep, 0)
        if k == 2:
            keep = jnp.where(row < 15, keep, 0)
        mats[k, 0, :, 0:48] = (rowi_ref[k].astype(F32) * keep.astype(F32)).astype(BF)
        mats[k, 1, :, 0:48] = coli_ref[k]
    gacc[...] = jnp.zeros_like(gacc)

    def chunk(t):
        rows = pl.ds(pl.multiple_of(t * CH, CH), CH)
        gain = gain_ref[...]

        @pl.loop(0, CH // 32)
        def _(s):
            r0 = pl.multiple_of(s * 32, 32)
            v = xv[pl.ds(pl.multiple_of(t * CH + r0, 32), 32), :].astype(F32)
            center = jnp.mean(v, -1, keepdims=True)
            sh = v - center
            inv = lax.rsqrt(jnp.mean(sh * sh, -1, keepdims=True) + EPS)
            nv = sh * inv
            normal[pl.ds(r0, 32), :] = nv
            inv_s[pl.ds(r0, 32), :] = jnp.broadcast_to(inv, (32, 128))
            normed[pl.ds(pl.multiple_of(t * CH + r0, 32), 32), :] = (nv * gain).astype(BF)

        @pl.loop(0, FF // FB)
        def _(f):
            cols = pl.ds(pl.multiple_of(f * FB, FB), FB)
            pre = nn(normed[rows, :], wu[:, cols])
            ba = nt(ct[rows, :], wd[cols, :])
            h = 0.5 * (1.0 + lax.erf(pre * ROOT_HALF))
            act[rows, cols] = (pre * h).astype(BF)
            bp[rows, cols] = (ba * (h + pre * jnp.exp(-0.5 * pre * pre) * INV_ROOT_TAU)).astype(BF)

        @pl.loop(0, D // FB)
        def _(f):
            cols = pl.ds(pl.multiple_of(f * FB, FB), FB)
            bn_s[:, cols] = nt(bp[rows, :], wu[cols, :])

        @pl.loop(0, CH // 32)
        def _(s):
            r0 = pl.multiple_of(s * 32, 32)
            r1 = pl.multiple_of(t * CH + r0, 32)
            bn = bn_s[pl.ds(r0, 32), :]
            nv = normal[pl.ds(r0, 32), :]
            inv = inv_s[pl.ds(r0, 32), 0:1]
            w = bn * nv
            gacc[...] += jnp.sum(w.reshape(4, 8, D), axis=0)
            scaled = bn * gain
            m1 = jnp.mean(scaled, -1, keepdims=True)
            m2 = jnp.mean(scaled * nv, -1, keepdims=True)
            g = ct[pl.ds(r1, 32), :].astype(F32) + inv * (scaled - m1 - nv * m2)
            gg[pl.ds(r1, 32), :] = g.astype(BF)

    def halo(t):
        rows = pl.ds(pl.multiple_of(t * CH, CH), CH)
        to_lower = pltpu.make_async_remote_copy(
            src_ref=gg.at[rows], dst_ref=ga_out.at[rows], send_sem=halo_send.at[0, t],
            recv_sem=halo_recv.at[0, t], device_id=lower, device_id_type=MESH)
        to_upper = pltpu.make_async_remote_copy(
            src_ref=gg.at[rows], dst_ref=gb_out.at[rows], send_sem=halo_send.at[1, t],
            recv_sem=halo_recv.at[1, t], device_id=upper, device_id_type=MESH)
        return to_lower, to_upper

    for cp in loads[:4]:
        cp.wait()
    chunk(0)
    pl.semaphore_wait(barrier, len(peers))
    m_low = remote(mats.at[0], mrecv.at[0], lower)
    m_upp = remote(mats.at[2], mrecv.at[1], upper)
    m_low.start()
    m_upp.start()
    for cp in halo(0):
        cp.start()
    for cp in loads[4:]:
        cp.wait()

    @pl.loop(1, NCH)
    def _(t):
        chunk(t)
        for cp in halo(t):
            cp.start()

    own = pltpu.make_async_copy(gg, gg_out, out_sem.at[0])
    own.start()

    gv = jnp.sum(gacc[...], axis=0, keepdims=True)
    gsrc[0] = jnp.concatenate([gv[:, 128 * i : 128 * (i + 1)] for i in range(8)], axis=0)
    g0 = remote(gsrc.at[0], grecv.at[0], pair)
    g0.start()

    order = [mod4(x + j) for j in (2, 1, 3, 0)]

    def up_tile(xq):
        feats = pl.ds(pl.multiple_of(xq * 256, 256), 256)

        @pl.loop(0, 4)
        def _(n):
            la = pl.ds(pl.multiple_of(n * 256, 256), 256)
            lb = pl.ds(pl.multiple_of(1024 + n * 256, 256), 256)
            left = tn(normed[:, feats], bp[:, la]).reshape(2, 16, 8, 256)
            right = tn(normed[:, feats], bp[:, lb]).reshape(2, 16, 8, 256)
            both = jnp.concatenate([left, right], axis=2).astype(BF)
            grad[0, pl.ds(2 * xq, 2), :, :, la] = both

    def down_tile(xq):
        hid = pl.ds(pl.multiple_of(xq * 512, 512), 512)

        @pl.loop(0, 4)
        def _(n):
            la = pl.ds(pl.multiple_of(n * 256, 256), 256)
            grad[1, pl.ds(2 * xq, 2), :, :, la] = (
                tn(act[:, hid], ct[:, la]).reshape(2, 16, 16, 256).astype(BF)
            )

    def add_into(dst, srcs, n):
        @pl.loop(0, n)
        def _(i):
            v = dst[i].astype(F32)
            for s in srcs:
                v = v + s[i].astype(F32)
            dst[i] = v.astype(BF)

    def add_to(out, srcs, n):
        @pl.loop(0, n)
        def _(i):
            v = srcs[0][i].astype(F32)
            for s in srcs[1:]:
                v = v + s[i].astype(F32)
            out[i] = v.astype(BF)

    xm, xp = mod4(x + 3), mod4(x + 1)
    ym, yp = mod4(y + 3), mod4(y + 1)
    zm, zp = mod4(z + 3), mod4(z + 1)
    p0 = [[None] * 4, [None] * 4]
    stage = [dict(), dict()]
    started = []

    def go(cp):
        cp.start()
        started.append(cp)
        return cp

    def tile(s, q):
        (up_tile if s == 0 else down_tile)(order[q])
        p0[s][q] = go(remote(grad.at[s, 2 * order[q] + (1 - c)], part.at[s, q], pair))

    def merge(s, q):
        p0[s][q].wait_recv()
        add_into(grad.at[s, 2 * order[q] + c], [part.at[s, q]], 16)

    def x_first(s):
        far = grad.at[s, 2 * order[0] + c]
        stage[s]["xa"] = [
            go(remote(far.at[pl.ds(0, 8)], xa.at[s, 0], dx(3))),
            go(remote(far.at[pl.ds(8, 8)], xa.at[s, 1], dx(1))),
        ]

    def x_second(s):
        low, high = grad.at[s, 2 * xm + c], grad.at[s, 2 * xp + c]
        stage[s]["xa"][0].wait_recv()
        add_into(low.at[pl.ds(0, 8)], [xa.at[s, 0]], 8)
        first = go(remote(low, xb.at[s, 0], dx(3)))
        stage[s]["xa"][1].wait_recv()
        add_into(high.at[pl.ds(8, 8)], [xa.at[s, 1]], 8)
        stage[s]["xb"] = [first, go(remote(high, xb.at[s, 1], dx(1)))]

    def x_done(s):
        for cp in stage[s]["xb"]:
            cp.wait_recv()
        add_to(tt.at[s], [grad.at[s, zone], xb.at[s, 0], xb.at[s, 1]], 16)

    def y_first(s):
        far = mod4(y + 2)
        stage[s]["ya"] = [
            go(remote(tt.at[s, pl.ds(4 * far, 2)], ya.at[s, 0], dy(3))),
            go(remote(tt.at[s, pl.ds(4 * far + 2, 2)], ya.at[s, 1], dy(1))),
        ]

    def y_second(s):
        stage[s]["ya"][0].wait_recv()
        add_into(tt.at[s, pl.ds(4 * ym, 2)], [ya.at[s, 0]], 2)
        first = go(remote(tt.at[s, pl.ds(4 * ym, 4)], yb.at[s, 0], dy(3)))
        stage[s]["ya"][1].wait_recv()
        add_into(tt.at[s, pl.ds(4 * yp + 2, 2)], [ya.at[s, 1]], 2)
        stage[s]["yb"] = [first, go(remote(tt.at[s, pl.ds(4 * yp, 4)], yb.at[s, 1], dy(1)))]

    def y_done(s):
        for cp in stage[s]["yb"]:
            cp.wait_recv()
        add_to(uu.at[s], [tt.at[s, pl.ds(4 * y, 4)], yb.at[s, 0], yb.at[s, 1]], 4)

    def z_first(s):
        far = uu.at[s, mod4(z + 2)]
        stage[s]["za"] = [
            go(remote(far.at[:, pl.ds(0, 512)], za.at[s, 0], dz(3))),
            go(remote(far.at[:, pl.ds(512, 512)], za.at[s, 1], dz(1))),
        ]

    def z_second(s):
        low, high = uu.at[s, zm], uu.at[s, zp]
        stage[s]["za"][0].wait_recv()
        low[:, 0:512] = (low[:, 0:512].astype(F32) + za[s, 0].astype(F32)).astype(BF)
        first = go(remote(low, zb.at[s, 0], dz(3)))
        stage[s]["za"][1].wait_recv()
        high[:, 512:1024] = (high[:, 512:1024].astype(F32) + za[s, 1].astype(F32)).astype(BF)
        stage[s]["zb"] = [first, go(remote(high, zb.at[s, 1], dz(1)))]

    def z_done(s):
        for cp in stage[s]["zb"]:
            cp.wait_recv()
        v = (uu[s, z].astype(F32) + zb[s, 0].astype(F32) + zb[s, 1].astype(F32)) * factor
        if s == 0:
            up_out[:, 0:1024] = v[0:8]
            up_out[:, 1024:2048] = v[8:16]
        else:
            down_out[...] = v

    gstage = {}

    def gain_send(axis_no, peer_of):
        gstage[axis_no] = [
            go(remote(gsrc.at[axis_no], grecv.at[3 * axis_no - 2 + j], peer_of(j + 1))) for j in range(3)
        ]

    def gain_sum(axis_no):
        v = gsrc[axis_no]
        for j, cp in enumerate(gstage[axis_no]):
            cp.wait_recv()
            v = v + grecv[3 * axis_no - 2 + j]
        gsrc[axis_no + 1] = v

    tile(0, 0)
    tile(0, 1)
    merge(0, 0)
    x_first(0)
    tile(0, 2)
    merge(0, 1)
    tile(0, 3)
    merge(0, 2)
    x_second(0)
    tile(1, 0)
    tile(1, 1)
    merge(1, 0)
    x_first(1)
    merge(0, 3)
    tile(1, 2)
    merge(1, 1)
    tile(1, 3)
    merge(1, 2)
    merge(1, 3)
    g0.wait_recv()
    gsrc[1] = gsrc[0] + grecv[0]
    gain_send(1, dx)
    x_second(1)
    gain_sum(1)
    gain_send(2, dy)
    x_done(0)
    y_first(0)
    gain_sum(2)
    gain_send(3, dz)
    y_second(0)
    y_done(0)
    z_first(0)
    gain_sum(3)
    z_second(0)
    x_done(1)
    y_first(1)
    z_done(0)
    y_second(1)
    y_done(1)
    z_first(1)
    z_second(1)
    z_done(1)

    sub = lax.broadcasted_iota(jnp.int32, (8, 128), 0)
    lane = lax.broadcasted_iota(jnp.int32, (8, 128), 1)
    line = jnp.sum(jnp.where(sub == zone, gsrc[4], 0.0), axis=0, keepdims=True)
    gain_out[...] = factor * jnp.sum(
        jnp.where(lane == 8 * row + sub, jnp.broadcast_to(line, (8, 128)), 0.0), axis=1, keepdims=True)

    m_low.wait()
    m_upp.wait()
    mats_out[0] = mrecv[0]
    mats_out[1] = mats[1]
    mats_out[2] = mrecv[1]
    for t in range(NCH):
        for cp in halo(t):
            cp.wait()
    own.wait()
    g0.wait_send()
    for cp in started:
        cp.wait_send()


def back(mats_ref, ga, gg, gb, out, b1, b2, half):
    @pl.when(pl.program_id(0) == 0)
    def _():
        r = lax.broadcasted_iota(jnp.int32, (384, 128), 0)
        q = lax.broadcasted_iota(jnp.int32, (384, 128), 1)
        pick_l = jnp.where(q == (r // 64) * 8 + r % 8, 1.0, 0.0).astype(BF)
        pick_m = jnp.where(q == r // 8, 1.0, 0.0).astype(BF)
        a = lax.broadcasted_iota(jnp.int32, (32, 256), 0)
        b = lax.broadcasted_iota(jnp.int32, (32, 256), 1)
        rep_j = jnp.where(b % 32 == a, 1.0, 0.0).astype(BF)
        rep_i = jnp.where(b // 8 == a, 1.0, 0.0).astype(BF)
        rr = lax.broadcasted_iota(jnp.int32, (384, 256), 0)
        cc = lax.broadcasted_iota(jnp.int32, (384, 256), 1)
        same_i = (rr // 8) % 8 == cc // 32
        same_l = rr % 8 == cc % 8
        for k in range(3):
            col = nt(pick_l, mats_ref[k, 1]).astype(BF)
            b1[k] = jnp.where(same_i, nn(col, rep_j), 0.0).astype(BF)
            rw = nt(pick_m, mats_ref[k, 0]).astype(BF)
            b2[:, k * 256 : (k + 1) * 256] = jnp.where(same_l, nn(rw, rep_i), 0.0).astype(BF)

    for k, src in enumerate((ga, gg, gb)):
        for g in range(4):
            h = nn(b1[k], src[g * 256 : (g + 1) * 256, :]).astype(BF)
            for lb in range(6):
                half[lb, k * 256 + g * 64 : k * 256 + (g + 1) * 64, :] = h[lb * 64 : (lb + 1) * 64]
    for lp in range(3):
        a = nn(b2[...], half[2 * lp]).reshape(48, 8, -1)
        b = nn(b2[...], half[2 * lp + 1]).reshape(48, 8, -1)
        out[:, lp * 16 : (lp + 1) * 16, :] = jnp.concatenate([a, b], axis=1).astype(BF)


def on_device(block_input, cotangent, w_up, w_down, ln_gain, pair_live, row_interp, col_interp):
    factor = 1.0 / math.sqrt(TOK * lax.axis_size("zone") * lax.axis_size("row"))
    hbm = pl.BlockSpec(memory_space=pl.ANY)
    vmem = pl.BlockSpec(memory_space=pltpu.VMEM)
    smem = pl.BlockSpec(memory_space=pltpu.SMEM)
    sds = jax.ShapeDtypeStruct
    grid_shape = sds((TOK, D), BF)
    gg, ga, gb, mats, up, down, gain = pl.pallas_call(
        functools.partial(front, factor),
        name="front",
        out_shape=(grid_shape, grid_shape, grid_shape, sds((3, 2, 32, 128), BF),
                   sds((8, FF), F32), sds((16, D), F32), sds((8, 1), F32)),
        in_specs=[smem, hbm, hbm, hbm, hbm, vmem, vmem, vmem],
        out_specs=(hbm, hbm, hbm, vmem, vmem, vmem, vmem),
        scratch_shapes=[
            pltpu.VMEM((TOK, D), BF),
            pltpu.VMEM((TOK, D), BF),
            pltpu.VMEM((D, FF), BF),
            pltpu.VMEM((FF, D), BF),
            pltpu.VMEM((TOK, D), BF),
            pltpu.VMEM((TOK, FF), BF),
            pltpu.VMEM((TOK, FF), BF),
            pltpu.VMEM((TOK, D), BF),
            pltpu.VMEM((CH, D), F32),
            pltpu.VMEM((CH, 128), F32),
            pltpu.VMEM((CH, D), F32),
            pltpu.VMEM((2, 8, 16, 16, 1024), BF),
            pltpu.VMEM((2, 4, 16, 16, 1024), BF),
            pltpu.VMEM((2, 2, 8, 16, 1024), BF),
            pltpu.VMEM((2, 2, 16, 16, 1024), BF),
            pltpu.VMEM((2, 16, 16, 1024), BF),
            pltpu.VMEM((2, 2, 2, 16, 1024), BF),
            pltpu.VMEM((2, 2, 4, 16, 1024), BF),
            pltpu.VMEM((2, 4, 16, 1024), BF),
            pltpu.VMEM((2, 2, 16, 512), BF),
            pltpu.VMEM((2, 2, 16, 1024), BF),
            pltpu.VMEM((3, 2, 32, 128), BF),
            pltpu.VMEM((2, 2, 32, 128), BF),
            pltpu.VMEM((8, D), F32),
            pltpu.VMEM((5, 8, 128), F32),
            pltpu.VMEM((10, 8, 128), F32),
            pltpu.SemaphoreType.DMA((6,)),
            pltpu.SemaphoreType.DMA((1,)),
            pltpu.SemaphoreType.DMA((N_SEM,)),
            pltpu.SemaphoreType.DMA((N_SEM,)),
            pltpu.SemaphoreType.DMA((2, NCH)),
            pltpu.SemaphoreType.DMA((2, NCH)),
        ],
        compiler_params=pltpu.CompilerParams(
            collective_id=0, has_side_effects=True, vmem_limit_bytes=60 * 1024 * 1024
        ),
    )(
        pair_live[0],
        block_input.reshape(TOK, D),
        cotangent.reshape(TOK, D),
        w_up,
        w_down,
        ln_gain.reshape(1, D),
        row_interp[0, 0],
        col_interp[0, 0],
    )
    lanes = 256
    source = pl.pallas_call(
        back,
        name="back",
        grid=(D // lanes,),
        out_shape=sds((48, 48, D), BF),
        in_specs=[pl.BlockSpec((3, 2, 32, 128), lambda i: (0, 0, 0, 0))]
        + [pl.BlockSpec((TOK, lanes), lambda i: (0, i))] * 3,
        out_specs=pl.BlockSpec((48, 48, lanes), lambda i: (0, 0, i)),
        scratch_shapes=[
            pltpu.VMEM((3, 384, 256), BF),
            pltpu.VMEM((384, 768), BF),
            pltpu.VMEM((6, 768, lanes), BF),
        ],
        compiler_params=pltpu.CompilerParams(dimension_semantics=("arbitrary",)),
    )(mats, ga, gg, gb)
    return source, up, down, gain.reshape(8)


def solution(mesh):
    in_specs = (
        P("row", "zone", None),
        P("row", "zone", None),
        P(),
        P(),
        P(),
        P("row", "zone", None),
        P("row", "zone", None, None, None),
        P("row", "zone", None, None, None),
    )
    out_specs = (
        P("row", "zone", None),
        P(("zone", "row"), None),
        P(("zone", "row"), None),
        P(("zone", "row")),
    )
    return jax.shard_map(
        on_device, mesh=mesh, in_specs=in_specs, out_specs=out_specs, check_vma=False
    )
```

time: 233 us -> 113 us (0.48)
  Pallas kernels: 0 us -> 110 us
  waiting for transfers between devices: 86.2 us -> 0 us
  matrix products: 66 us -> 0 us
  local copies, waits for them, and re-layouts: 21.6 us -> 1.27 us
  starting transfers between devices: 17.2 us -> 0 us
  between operations: 15.4 us -> 0.67 us
  blocking collectives: 13.5 us -> 0 us
  other arithmetic: 12 us -> 0.63 us
    pallas_call x0 -> x2, Pallas kernels: none -> 110 us  [the longest x1 99.5 us: on_device(): pl.pallas_call(functools.partial(front, factor), name='front', out_shape=...]
    unnamed x4 -> x0, waiting for transfers between devices: 78.8 us -> none
    dot_general x11 -> x0, matrix products: 66 us -> none  [the longest x3 23.5 us: pull_back(): jnp.einsum('im,ilc->mlc', rows_live, half, preferred_element_type=jnp.flo...]
    ppermute x6 -> x0, starting transfers between devices: 16.9 us -> none  [shifted_2(): lax.ppermute(value, axis, [(source, source + steps) for source in range(i...]
    unnamed x1 -> x0, blocking collectives: 13.5 us -> none
    unnamed x32 -> x8, local copies, waits for them, and re-layouts: 12.8 us -> 1.27 us
    ppermute x6 -> x0, waiting for transfers between devices: 7.39 us -> none  [shifted_2(): lax.ppermute(value, axis, [(source, source + steps) for source in range(i...]
    convert_element_type x5 -> x0, other arithmetic: 5.02 us -> none  [the longest x1 3.03 us: on_device(): grid_block = grad_in.astype(jnp.bfloat16).reshape(side, side, width)]
  transfers between devices with their start and end apart: 9 -> 0, of which waited for: 3 -> 0; matrix products, arithmetic and copies ran while one was open for 32% -> 0% of each run, Pallas kernels for 0% -> 0%
where the time goes in v1:
time: 113 us
  Pallas kernels  110 us (97%)
  local copies, waits for them, and re-layouts  1.27 us (1%)
    pallas_call x1, Pallas kernels, on_device(): pl.pallas_call(functools.partial(front, factor), name='front', out_shape=...  99.5 us
    pallas_call x1, Pallas kernels, on_device(): pl.pallas_call(back, name='back', grid=(D // lanes,), out_shape=sds((48,...  10.5 us

profile of v1, /device:TPU:0, one launch (start us, length us, event | category | flops | bytes accessed | tf_op | source)
XLA Modules:
  0.0 112.5 jit_solution(510924915533917776)
XLA Ops:
  0.6 99.5 %front.1 = (bf16[1024,1024]{1,0:T(8,128)(2,1)}, bf16[1024,1024]{1,0:T(8,128)(2,1)}, bf16[1024,1024]{1,0:T(8,128)(2,1)}, bf16[3,2,32,128]{3,2,1,0:T(8,128)(2,1)},...) custom-call(s32[1,3]{1,0:T(1,128)} %bitcast.11, bf16[1024,1024]{1,0:T(8,128)(2,1)} %bitcast.6, ...), custom_call_target="tpu_custom_call" | custom-call | tf_op jit(solution)/shard_map/front/pallas_call | solution.py:473
  100.2 0.0 copy-start.2
  100.2 0.0 copy-start.1
  100.2 0.0 copy-start
  100.2 10.5 %back.1 = bf16[48,48,1024]{2,1,0:T(8,128)(2,1)} custom-call(bf16[3,2,32,128]{3,2,1,0:T(8,128)(2,1)} %get-tuple-element.11.mats_ref, bf16[1024,1024]{1,0:T(8,128)(2,1)} %get-tuple-element.12.ga, bf16[1024,1024]{1,0:T(8,128)(2,1)} %get-tuple-element.13.gg, bf16[1024,1024]{1,0:T(8,128)(2,1)} %get-tuple-element.14.gb), custom_call_target="tpu_custom_call" | custom-call | tf_op jit(solution)/shard_map/back/pallas_call | solution.py:528
  110.7 0.0 copy-done.2
  110.7 0.6 reduce
  111.3 0.0 copy-done.1
  111.3 0.6 copy.14
  111.9 0.0 copy-done
  111.9 0.6 copy.15
Async XLA Ops:
  100.2 10.5 %copy-start.2 = (f32[8,1]{1,0:T(8,128)S(1)}, f32[8,1]{1,0:T(8,128)}, u32[]{:S(2)}) copy-start(f32[8,1]{1,0:T(8,128)} %get-tuple-element.17) | copy-start | bytes 100
  100.2 11.1 %copy-start.1 = (f32[8,2048]{1,0:T(8,128)S(1)}, f32[8,2048]{1,0:T(8,128)}, u32[]{:S(2)}) copy-start(f32[8,2048]{1,0:T(8,128)} %get-tuple-element.23) | copy-start | bytes 196612
  100.2 11.7 %copy-start = (f32[16,1024]{1,0:T(8,128)S(1)}, f32[16,1024]{1,0:T(8,128)}, u32[]{:S(2)}) copy-start(f32[16,1024]{1,0:T(8,128)} %get-tuple-element.24) | copy-start | bytes 196612

commit v2 on v1

--- a/solution.py
+++ b/solution.py
@@ -19,7 +19,9 @@
 TOK = 1024
 CH = 256
 NCH = TOK // CH
-FB = 512
+FB = 1024
+NB = 1024
+LN = 512
 N_SEM = 64
 
 
@@ -57,7 +59,8 @@
     wu,
     wd,
     normed,
-    act,
+    normed_t,
+    act_t,
     bp,
     gg,
     normal,
@@ -145,53 +148,55 @@
         mats[k, 1, :, 0:48] = coli_ref[k]
     gacc[...] = jnp.zeros_like(gacc)
 
-    def chunk(t):
-        rows = pl.ds(pl.multiple_of(t * CH, CH), CH)
+    def forward(start, m):
         gain = gain_ref[...]
-
-        @pl.loop(0, CH // 32)
-        def _(s):
-            r0 = pl.multiple_of(s * 32, 32)
-            v = xv[pl.ds(pl.multiple_of(t * CH + r0, 32), 32), :].astype(F32)
+        base = start % 512
+
+        for s in range(m // CH):
+            r0, r1 = base + s * CH, start + s * CH
+            v = xv[r1 : r1 + CH, :].astype(F32)
             center = jnp.mean(v, -1, keepdims=True)
             sh = v - center
             inv = lax.rsqrt(jnp.mean(sh * sh, -1, keepdims=True) + EPS)
             nv = sh * inv
-            normal[pl.ds(r0, 32), :] = nv
-            inv_s[pl.ds(r0, 32), :] = jnp.broadcast_to(inv, (32, 128))
-            normed[pl.ds(pl.multiple_of(t * CH + r0, 32), 32), :] = (nv * gain).astype(BF)
+            normal[r0 : r0 + CH, :] = nv
+            inv_s[r0 : r0 + CH, :] = jnp.broadcast_to(inv, (CH, 128))
+            nb = (nv * gain).astype(BF)
+            normed[r0 : r0 + CH, :] = nb
+            normed_t[:, r1 : r1 + CH] = nb.T
 
         @pl.loop(0, FF // FB)
         def _(f):
             cols = pl.ds(pl.multiple_of(f * FB, FB), FB)
-            pre = nn(normed[rows, :], wu[:, cols])
-            ba = nt(ct[rows, :], wd[cols, :])
+            pre = nn(normed[base : base + m, :], wu[:, cols])
+            ba = nt(ct[start : start + m, :], wd[cols, :])
             h = 0.5 * (1.0 + lax.erf(pre * ROOT_HALF))
-            act[rows, cols] = (pre * h).astype(BF)
-            bp[rows, cols] = (ba * (h + pre * jnp.exp(-0.5 * pre * pre) * INV_ROOT_TAU)).astype(BF)
-
-        @pl.loop(0, D // FB)
+            act_t[cols, start : start + m] = (pre * h).astype(BF).T
+            bp[start : start + m, cols] = (
+                ba * (h + pre * jnp.exp(-0.5 * pre * pre) * INV_ROOT_TAU)
+            ).astype(BF)
+
+    def backward(start):
+        gain = gain_ref[...]
+        base = start % 512
+
+        @pl.loop(0, D // NB)
         def _(f):
-            cols = pl.ds(pl.multiple_of(f * FB, FB), FB)
-            bn_s[:, cols] = nt(bp[rows, :], wu[cols, :])
-
-        @pl.loop(0, CH // 32)
-        def _(s):
-            r0 = pl.multiple_of(s * 32, 32)
-            r1 = pl.multiple_of(t * CH + r0, 32)
-            bn = bn_s[pl.ds(r0, 32), :]
-            nv = normal[pl.ds(r0, 32), :]
-            inv = inv_s[pl.ds(r0, 32), 0:1]
-            w = bn * nv
-            gacc[...] += jnp.sum(w.reshape(4, 8, D), axis=0)
-            scaled = bn * gain
-            m1 = jnp.mean(scaled, -1, keepdims=True)
-            m2 = jnp.mean(scaled * nv, -1, keepdims=True)
-            g = ct[pl.ds(r1, 32), :].astype(F32) + inv * (scaled - m1 - nv * m2)
-            gg[pl.ds(r1, 32), :] = g.astype(BF)
+            cols = pl.ds(pl.multiple_of(f * NB, NB), NB)
+            bn_s[:, cols] = nt(bp[start : start + CH, :], wu[cols, :])
+
+        bn = bn_s[...]
+        nv = normal[base : base + CH, :]
+        inv = inv_s[base : base + CH, 0:1]
+        gacc[...] += jnp.sum((bn * nv).reshape(CH // 8, 8, D), axis=0)
+        scaled = bn * gain
+        m1 = jnp.mean(scaled, -1, keepdims=True)
+        m2 = jnp.mean(scaled * nv, -1, keepdims=True)
+        g = ct[start : start + CH, :].astype(F32) + inv * (scaled - m1 - nv * m2)
+        gg[start : start + CH, :] = g.astype(BF)
 
     def halo(t):
-        rows = pl.ds(pl.multiple_of(t * CH, CH), CH)
+        rows = pl.ds(t * CH, CH)
         to_lower = pltpu.make_async_remote_copy(
             src_ref=gg.at[rows], dst_ref=ga_out.at[rows], send_sem=halo_send.at[0, t],
             recv_sem=halo_recv.at[0, t], device_id=lower, device_id_type=MESH)
@@ -202,7 +207,8 @@
 
     for cp in loads[:4]:
         cp.wait()
-    chunk(0)
+    forward(0, CH)
+    backward(0)
     pl.semaphore_wait(barrier, len(peers))
     m_low = remote(mats.at[0], mrecv.at[0], lower)
     m_upp = remote(mats.at[2], mrecv.at[1], upper)
@@ -212,43 +218,37 @@
         cp.start()
     for cp in loads[4:]:
         cp.wait()
-
-    @pl.loop(1, NCH)
-    def _(t):
-        chunk(t)
-        for cp in halo(t):
-            cp.start()
-
-    own = pltpu.make_async_copy(gg, gg_out, out_sem.at[0])
-    own.start()
-
-    gv = jnp.sum(gacc[...], axis=0, keepdims=True)
-    gsrc[0] = jnp.concatenate([gv[:, 128 * i : 128 * (i + 1)] for i in range(8)], axis=0)
-    g0 = remote(gsrc.at[0], grecv.at[0], pair)
-    g0.start()
+    forward(CH, CH)
+    backward(CH)
+    for cp in halo(1):
+        cp.start()
+    forward(2 * CH, 2 * CH)
 
     order = [mod4(x + j) for j in (2, 1, 3, 0)]
 
-    def up_tile(xq):
-        feats = pl.ds(pl.multiple_of(xq * 256, 256), 256)
-
-        @pl.loop(0, 4)
+    def up_tiles(xa_, xb_):
+        fa = pl.ds(pl.multiple_of(xa_ * 256, 256), 256)
+        fb = pl.ds(pl.multiple_of(xb_ * 256, 256), 256)
+
+        @pl.loop(0, 1024 // LN)
         def _(n):
-            la = pl.ds(pl.multiple_of(n * 256, 256), 256)
-            lb = pl.ds(pl.multiple_of(1024 + n * 256, 256), 256)
-            left = tn(normed[:, feats], bp[:, la]).reshape(2, 16, 8, 256)
-            right = tn(normed[:, feats], bp[:, lb]).reshape(2, 16, 8, 256)
+            la = pl.ds(pl.multiple_of(n * LN, LN), LN)
+            lb = pl.ds(pl.multiple_of(1024 + n * LN, LN), LN)
+            lhs = jnp.concatenate([normed_t[fa, :], normed_t[fb, :]], axis=0)
+            left = nn(lhs, bp[:, la]).reshape(4, 16, 8, LN)
+            right = nn(lhs, bp[:, lb]).reshape(4, 16, 8, LN)
             both = jnp.concatenate([left, right], axis=2).astype(BF)
-            grad[0, pl.ds(2 * xq, 2), :, :, la] = both
+            grad[0, pl.ds(2 * xa_, 2), :, :, la] = both[0:2]
+            grad[0, pl.ds(2 * xb_, 2), :, :, la] = both[2:4]
 
     def down_tile(xq):
         hid = pl.ds(pl.multiple_of(xq * 512, 512), 512)
 
-        @pl.loop(0, 4)
+        @pl.loop(0, 1024 // LN)
         def _(n):
-            la = pl.ds(pl.multiple_of(n * 256, 256), 256)
+            la = pl.ds(pl.multiple_of(n * LN, LN), LN)
             grad[1, pl.ds(2 * xq, 2), :, :, la] = (
-                tn(act[:, hid], ct[:, la]).reshape(2, 16, 16, 256).astype(BF)
+                nn(act_t[hid, :], ct[:, la]).reshape(2, 16, 16, LN).astype(BF)
             )
 
     def add_into(dst, srcs, n):
@@ -279,8 +279,7 @@
         started.append(cp)
         return cp
 
-    def tile(s, q):
-        (up_tile if s == 0 else down_tile)(order[q])
+    def send_pair(s, q):
         p0[s][q] = go(remote(grad.at[s, 2 * order[q] + (1 - c)], part.at[s, q], pair))
 
     def merge(s, q):
@@ -368,29 +367,47 @@
             v = v + grecv[3 * axis_no - 2 + j]
         gsrc[axis_no + 1] = v
 
-    tile(0, 0)
-    tile(0, 1)
+    up_tiles(order[0], order[1])
+    send_pair(0, 0)
+    send_pair(0, 1)
+    up_tiles(order[2], order[3])
+    send_pair(0, 2)
+    send_pair(0, 3)
     merge(0, 0)
     x_first(0)
-    tile(0, 2)
+    backward(2 * CH)
+    for cp in halo(2):
+        cp.start()
     merge(0, 1)
-    tile(0, 3)
     merge(0, 2)
     x_second(0)
-    tile(1, 0)
-    tile(1, 1)
+    down_tile(order[0])
+    send_pair(1, 0)
+    down_tile(order[1])
+    send_pair(1, 1)
+    merge(0, 3)
     merge(1, 0)
     x_first(1)
-    merge(0, 3)
-    tile(1, 2)
+    down_tile(order[2])
+    send_pair(1, 2)
+    down_tile(order[3])
+    send_pair(1, 3)
     merge(1, 1)
-    tile(1, 3)
+    backward(3 * CH)
+    for cp in halo(3):
+        cp.start()
+    own = pltpu.make_async_copy(gg, gg_out, out_sem.at[0])
+    own.start()
+    gv = jnp.sum(gacc[...], axis=0, keepdims=True)
+    gsrc[0] = jnp.concatenate([gv[:, 128 * i : 128 * (i + 1)] for i in range(8)], axis=0)
+    g0 = remote(gsrc.at[0], grecv.at[0], pair)
+    g0.start()
     merge(1, 2)
     merge(1, 3)
+    x_second(1)
     g0.wait_recv()
     gsrc[1] = gsrc[0] + grecv[0]
     gain_send(1, dx)
-    x_second(1)
     gain_sum(1)
     gain_send(2, dy)
     x_done(0)
@@ -482,12 +499,13 @@
             pltpu.VMEM((TOK, D), BF),
             pltpu.VMEM((D, FF), BF),
             pltpu.VMEM((FF, D), BF),
-            pltpu.VMEM((TOK, D), BF),
-            pltpu.VMEM((TOK, FF), BF),
+            pltpu.VMEM((512, D), BF),
+            pltpu.VMEM((D, TOK), BF),
+            pltpu.VMEM((FF, TOK), BF),
             pltpu.VMEM((TOK, FF), BF),
             pltpu.VMEM((TOK, D), BF),
-            pltpu.VMEM((CH, D), F32),
-            pltpu.VMEM((CH, 128), F32),
+            pltpu.VMEM((512, D), F32),
+            pltpu.VMEM((512, 128), F32),
             pltpu.VMEM((CH, D), F32),
             pltpu.VMEM((2, 8, 16, 16, 1024), BF),
             pltpu.VMEM((2, 4, 16, 16, 1024), BF),

time: 113 us -> 113 us (level)
  no operation moved by 1% of the time
where the time goes in v2:
time: 113 us; the launch traced here: 112 us
  Pallas kernels  110 us (97%)
  local copies, waits for them, and re-layouts  1.27 us (1%)
    pallas_call x1, Pallas kernels, on_device(): pl.pallas_call(functools.partial(front, factor), name='front', out_shape=...  99.4 us
    pallas_call x1, Pallas kernels, on_device(): pl.pallas_call(back, name='back', grid=(D // lanes,), out_shape=sds((48,...  10.5 us

profile of v2, /device:TPU:0, one launch (start us, length us, event | category | flops | bytes accessed | tf_op | source)
XLA Modules:
  0.0 112.4 jit_solution(17314920608874798679)
XLA Ops:
  0.6 99.4 %front.1 = (bf16[1024,1024]{1,0:T(8,128)(2,1)}, bf16[1024,1024]{1,0:T(8,128)(2,1)}, bf16[1024,1024]{1,0:T(8,128)(2,1)}, bf16[3,2,32,128]{3,2,1,0:T(8,128)(2,1)},...) custom-call(s32[1,3]{1,0:T(1,128)} %bitcast.11, bf16[1024,1024]{1,0:T(8,128)(2,1)} %bitcast.6, ...), custom_call_target="tpu_custom_call" | custom-call | tf_op jit(solution)/shard_map/front/pallas_call | solution.py:490
  100.0 0.0 copy-start.2
  100.0 0.0 copy-start.1
  100.0 0.0 copy-start
  100.0 10.5 %back.1 = bf16[48,48,1024]{2,1,0:T(8,128)(2,1)} custom-call(bf16[3,2,32,128]{3,2,1,0:T(8,128)(2,1)} %get-tuple-element.11.mats_ref, bf16[1024,1024]{1,0:T(8,128)(2,1)} %get-tuple-element.12.ga, bf16[1024,1024]{1,0:T(8,128)(2,1)} %get-tuple-element.13.gg, bf16[1024,1024]{1,0:T(8,128)(2,1)} %get-tuple-element.14.gb), custom_call_target="tpu_custom_call" | custom-call | tf_op jit(solution)/shard_map/back/pallas_call | solution.py:546
  110.5 0.0 copy-done.2
  110.5 0.6 reduce
  111.1 0.0 copy-done.1
  111.1 0.6 copy.14
  111.8 0.0 copy-done
  111.8 0.6 copy.15
Async XLA Ops:
  100.0 10.5 %copy-start.2 = (f32[8,1]{1,0:T(8,128)S(1)}, f32[8,1]{1,0:T(8,128)}, u32[]{:S(2)}) copy-start(f32[8,1]{1,0:T(8,128)} %get-tuple-element.17) | copy-start | bytes 100
  100.0 11.1 %copy-start.1 = (f32[8,2048]{1,0:T(8,128)S(1)}, f32[8,2048]{1,0:T(8,128)}, u32[]{:S(2)}) copy-start(f32[8,2048]{1,0:T(8,128)} %get-tuple-element.23) | copy-start | bytes 196612
  100.0 11.7 %copy-start = (f32[16,1024]{1,0:T(8,128)S(1)}, f32[16,1024]{1,0:T(8,128)}, u32[]{:S(2)}) copy-start(f32[16,1024]{1,0:T(8,128)} %get-tuple-element.24) | copy-start | bytes 196612

commit v3 on v2

--- a/solution.py
+++ b/solution.py
@@ -23,6 +23,7 @@
 NB = 1024
 LN = 512
 N_SEM = 64
+N_RELAY = 2
 
 
 def nt(a, b):
@@ -87,6 +88,9 @@
     recv_sem,
     halo_send,
     halo_recv,
+    relay,
+    relay_send,
+    relay_recv,
 ):
     zone = lax.axis_index("zone")
     row = lax.axis_index("row")
@@ -171,7 +175,7 @@
             pre = nn(normed[base : base + m, :], wu[:, cols])
             ba = nt(ct[start : start + m, :], wd[cols, :])
             h = 0.5 * (1.0 + lax.erf(pre * ROOT_HALF))
-            act_t[cols, start : start + m] = (pre * h).astype(BF).T
+            act_t[pl.ds(4 * f, 4), :, :, start : start + m] = (pre * h).astype(BF).T.reshape(4, 4, 64, m)
             bp[start : start + m, cols] = (
                 ba * (h + pre * jnp.exp(-0.5 * pre * pre) * INV_ROOT_TAU)
             ).astype(BF)
@@ -195,15 +199,63 @@
         g = ct[start : start + CH, :].astype(F32) + inv * (scaled - m1 - nv * m2)
         gg[start : start + CH, :] = g.astype(BF)
 
+    def tokens(t):
+        return pl.ds(t * CH, CH)
+
+    def hop(src, dst, send, recv, device):
+        return pltpu.make_async_remote_copy(
+            src_ref=src, dst_ref=dst, send_sem=send, recv_sem=recv,
+            device_id=device, device_id_type=MESH)
+
     def halo(t):
-        rows = pl.ds(t * CH, CH)
-        to_lower = pltpu.make_async_remote_copy(
-            src_ref=gg.at[rows], dst_ref=ga_out.at[rows], send_sem=halo_send.at[0, t],
-            recv_sem=halo_recv.at[0, t], device_id=lower, device_id_type=MESH)
-        to_upper = pltpu.make_async_remote_copy(
-            src_ref=gg.at[rows], dst_ref=gb_out.at[rows], send_sem=halo_send.at[1, t],
-            recv_sem=halo_recv.at[1, t], device_id=upper, device_id_type=MESH)
-        return to_lower, to_upper
+        src = gg.at[tokens(t)]
+        return (
+            hop(src, ga_out.at[tokens(t)], halo_send.at[0, t], halo_recv.at[0, t], lower),
+            hop(src, gb_out.at[tokens(t)], halo_send.at[1, t], halo_recv.at[1, t], upper),
+        )
+
+    def halo_start(t):
+        src = gg.at[tokens(t)]
+        to_lower, to_upper = halo(t)
+        if t >= N_RELAY:
+            to_lower.start()
+            to_upper.start()
+            return
+
+        @pl.when(z > 0)
+        def _():
+            to_lower.start()
+
+        @pl.when(z == 0)
+        def _():
+            hop(src, relay.at[t], halo_send.at[0, t], relay_recv.at[t], dz(3)).start()
+
+        @pl.when(z < 3)
+        def _():
+            to_upper.start()
+
+        @pl.when(z == 3)
+        def _():
+            hop(src, relay.at[t], halo_send.at[1, t], relay_recv.at[t], dz(1)).start()
+
+    def relays(t):
+        down = hop(relay.at[t], ga_out.at[tokens(t)], relay_send.at[t], halo_recv.at[0, t], dy(3))
+        up = hop(relay.at[t], gb_out.at[tokens(t)], relay_send.at[t], halo_recv.at[1, t], dy(1))
+        land = hop(relay.at[t], relay.at[t], relay_send.at[t], relay_recv.at[t], dz(1))
+        return down, up, land
+
+    def relay_step(t):
+        down, up, land = relays(t)
+
+        @pl.when(z == 0)
+        def _():
+            land.wait_recv()
+            up.start()
+
+        @pl.when(z == 3)
+        def _():
+            land.wait_recv()
+            down.start()
 
     for cp in loads[:4]:
         cp.wait()
@@ -214,50 +266,42 @@
     m_upp = remote(mats.at[2], mrecv.at[1], upper)
     m_low.start()
     m_upp.start()
-    for cp in halo(0):
-        cp.start()
+    halo_start(0)
     for cp in loads[4:]:
         cp.wait()
     forward(CH, CH)
     backward(CH)
-    for cp in halo(1):
-        cp.start()
+    halo_start(1)
     forward(2 * CH, 2 * CH)
 
-    order = [mod4(x + j) for j in (2, 1, 3, 0)]
-
-    def up_tiles(xa_, xb_):
-        fa = pl.ds(pl.multiple_of(xa_ * 256, 256), 256)
-        fb = pl.ds(pl.multiple_of(xb_ * 256, 256), 256)
+    at = ((x, y), (y, x))
+    to = ((dx, dy), (dy, dx))
+    order = [[mod4(at[s][0] + j) for j in (2, 1, 3, 0)] for s in range(2)]
+
+    def up_tiles(ta, tb):
+        fa = pl.ds(pl.multiple_of(ta * 256, 256), 256)
+        fb = pl.ds(pl.multiple_of(tb * 256, 256), 256)
 
         @pl.loop(0, 1024 // LN)
         def _(n):
             la = pl.ds(pl.multiple_of(n * LN, LN), LN)
             lb = pl.ds(pl.multiple_of(1024 + n * LN, LN), LN)
             lhs = jnp.concatenate([normed_t[fa, :], normed_t[fb, :]], axis=0)
-            left = nn(lhs, bp[:, la]).reshape(4, 16, 8, LN)
-            right = nn(lhs, bp[:, lb]).reshape(4, 16, 8, LN)
-            both = jnp.concatenate([left, right], axis=2).astype(BF)
-            grad[0, pl.ds(2 * xa_, 2), :, :, la] = both[0:2]
-            grad[0, pl.ds(2 * xb_, 2), :, :, la] = both[2:4]
-
-    def down_tile(xq):
-        hid = pl.ds(pl.multiple_of(xq * 512, 512), 512)
-
+            left = nn(lhs, bp[:, la]).reshape(2, 2, 4, 4, 8, LN)
+            right = nn(lhs, bp[:, lb]).reshape(2, 2, 4, 4, 8, LN)
+            both = jnp.concatenate([left, right], axis=4).astype(BF)
+            for cc in range(2):
+                grad[0, cc, ta, :, :, :, la] = both[0, cc]
+                grad[0, cc, tb, :, :, :, la] = both[1, cc]
+
+    def down_tile(ty):
         @pl.loop(0, 1024 // LN)
         def _(n):
             la = pl.ds(pl.multiple_of(n * LN, LN), LN)
-            grad[1, pl.ds(2 * xq, 2), :, :, la] = (
-                nn(act_t[hid, :], ct[:, la]).reshape(2, 16, 16, LN).astype(BF)
-            )
-
-    def add_into(dst, srcs, n):
-        @pl.loop(0, n)
-        def _(i):
-            v = dst[i].astype(F32)
-            for s in srcs:
-                v = v + s[i].astype(F32)
-            dst[i] = v.astype(BF)
+            v = nn(act_t[:, ty].reshape(512, TOK), ct[:, la])
+            v = v.reshape(4, 2, 4, 16, LN).astype(BF)
+            for cc in range(2):
+                grad[1, cc, ty, :, :, :, la] = v[:, cc]
 
     def add_to(out, srcs, n):
         @pl.loop(0, n)
@@ -267,8 +311,9 @@
                 v = v + s[i].astype(F32)
             out[i] = v.astype(BF)
 
-    xm, xp = mod4(x + 3), mod4(x + 1)
-    ym, yp = mod4(y + 3), mod4(y + 1)
+    def add_into(dst, src, n):
+        add_to(dst, [dst, src], n)
+
     zm, zp = mod4(z + 3), mod4(z + 1)
     p0 = [[None] * 4, [None] * 4]
     stage = [dict(), dict()]
@@ -280,52 +325,56 @@
         return cp
 
     def send_pair(s, q):
-        p0[s][q] = go(remote(grad.at[s, 2 * order[q] + (1 - c)], part.at[s, q], pair))
+        p0[s][q] = go(remote(grad.at[s, 1 - c, order[s][q]], part.at[s, q], pair))
 
     def merge(s, q):
         p0[s][q].wait_recv()
-        add_into(grad.at[s, 2 * order[q] + c], [part.at[s, q]], 16)
-
-    def x_first(s):
-        far = grad.at[s, 2 * order[0] + c]
-        stage[s]["xa"] = [
-            go(remote(far.at[pl.ds(0, 8)], xa.at[s, 0], dx(3))),
-            go(remote(far.at[pl.ds(8, 8)], xa.at[s, 1], dx(1))),
+        add_into(grad.at[s, c, order[s][q]], part.at[s, q], 4)
+
+    def a_first(s):
+        far = grad.at[s, c, order[s][0]]
+        peer = to[s][0]
+        stage[s]["a1"] = [
+            go(remote(far.at[pl.ds(0, 2)], xa.at[s, 0], peer(3))),
+            go(remote(far.at[pl.ds(2, 2)], xa.at[s, 1], peer(1))),
         ]
 
-    def x_second(s):
-        low, high = grad.at[s, 2 * xm + c], grad.at[s, 2 * xp + c]
-        stage[s]["xa"][0].wait_recv()
-        add_into(low.at[pl.ds(0, 8)], [xa.at[s, 0]], 8)
-        first = go(remote(low, xb.at[s, 0], dx(3)))
-        stage[s]["xa"][1].wait_recv()
-        add_into(high.at[pl.ds(8, 8)], [xa.at[s, 1]], 8)
-        stage[s]["xb"] = [first, go(remote(high, xb.at[s, 1], dx(1)))]
-
-    def x_done(s):
-        for cp in stage[s]["xb"]:
+    def a_second(s):
+        low, high = grad.at[s, c, order[s][2]], grad.at[s, c, order[s][1]]
+        peer = to[s][0]
+        stage[s]["a1"][0].wait_recv()
+        add_into(low.at[pl.ds(0, 2)], xa.at[s, 0], 2)
+        first = go(remote(low, xb.at[s, 0], peer(3)))
+        stage[s]["a1"][1].wait_recv()
+        add_into(high.at[pl.ds(2, 2)], xa.at[s, 1], 2)
+        stage[s]["a2"] = [first, go(remote(high, xb.at[s, 1], peer(1)))]
+
+    def a_done(s):
+        for cp in stage[s]["a2"]:
             cp.wait_recv()
-        add_to(tt.at[s], [grad.at[s, zone], xb.at[s, 0], xb.at[s, 1]], 16)
-
-    def y_first(s):
-        far = mod4(y + 2)
-        stage[s]["ya"] = [
-            go(remote(tt.at[s, pl.ds(4 * far, 2)], ya.at[s, 0], dy(3))),
-            go(remote(tt.at[s, pl.ds(4 * far + 2, 2)], ya.at[s, 1], dy(1))),
+        add_to(tt.at[s], [grad.at[s, c, order[s][3]], xb.at[s, 0], xb.at[s, 1]], 4)
+
+    def b_first(s):
+        far, peer = tt.at[s, mod4(at[s][1] + 2)], to[s][1]
+        stage[s]["b1"] = [
+            go(remote(far.at[pl.ds(0, 2)], ya.at[s, 0], peer(3))),
+            go(remote(far.at[pl.ds(2, 2)], ya.at[s, 1], peer(1))),
         ]
 
-    def y_second(s):
-        stage[s]["ya"][0].wait_recv()
-        add_into(tt.at[s, pl.ds(4 * ym, 2)], [ya.at[s, 0]], 2)
-        first = go(remote(tt.at[s, pl.ds(4 * ym, 4)], yb.at[s, 0], dy(3)))
-        stage[s]["ya"][1].wait_recv()
-        add_into(tt.at[s, pl.ds(4 * yp + 2, 2)], [ya.at[s, 1]], 2)
-        stage[s]["yb"] = [first, go(remote(tt.at[s, pl.ds(4 * yp, 4)], yb.at[s, 1], dy(1)))]
-
-    def y_done(s):
-        for cp in stage[s]["yb"]:
+    def b_second(s):
+        low, high = tt.at[s, mod4(at[s][1] + 3)], tt.at[s, mod4(at[s][1] + 1)]
+        peer = to[s][1]
+        stage[s]["b1"][0].wait_recv()
+        add_into(low.at[pl.ds(0, 2)], ya.at[s, 0], 2)
+        first = go(remote(low, yb.at[s, 0], peer(3)))
+        stage[s]["b1"][1].wait_recv()
+        add_into(high.at[pl.ds(2, 2)], ya.at[s, 1], 2)
+        stage[s]["b2"] = [first, go(remote(high, yb.at[s, 1], peer(1)))]
+
+    def b_done(s):
+        for cp in stage[s]["b2"]:
             cp.wait_recv()
-        add_to(uu.at[s], [tt.at[s, pl.ds(4 * y, 4)], yb.at[s, 0], yb.at[s, 1]], 4)
+        add_to(uu.at[s], [tt.at[s, at[s][1]], yb.at[s, 0], yb.at[s, 1]], 4)
 
     def z_first(s):
         far = uu.at[s, mod4(z + 2)]
@@ -367,65 +416,65 @@
             v = v + grecv[3 * axis_no - 2 + j]
         gsrc[axis_no + 1] = v
 
-    up_tiles(order[0], order[1])
+    up_tiles(order[0][0], order[0][1])
     send_pair(0, 0)
     send_pair(0, 1)
-    up_tiles(order[2], order[3])
+    down_tile(order[1][0])
+    send_pair(1, 0)
+    merge(0, 0)
+    a_first(0)
+    down_tile(order[1][1])
+    send_pair(1, 1)
+    merge(1, 0)
+    a_first(1)
+    relay_step(0)
+    up_tiles(order[0][2], order[0][3])
     send_pair(0, 2)
     send_pair(0, 3)
-    merge(0, 0)
-    x_first(0)
+    merge(0, 1)
+    merge(1, 1)
     backward(2 * CH)
-    for cp in halo(2):
-        cp.start()
-    merge(0, 1)
+    halo_start(2)
     merge(0, 2)
-    x_second(0)
-    down_tile(order[0])
-    send_pair(1, 0)
-    down_tile(order[1])
-    send_pair(1, 1)
+    a_second(0)
+    down_tile(order[1][2])
+    send_pair(1, 2)
+    down_tile(order[1][3])
+    send_pair(1, 3)
     merge(0, 3)
-    merge(1, 0)
-    x_first(1)
-    down_tile(order[2])
-    send_pair(1, 2)
-    down_tile(order[3])
-    send_pair(1, 3)
-    merge(1, 1)
+    merge(1, 2)
+    a_second(1)
+    relay_step(1)
     backward(3 * CH)
-    for cp in halo(3):
-        cp.start()
+    halo_start(3)
+    merge(1, 3)
     own = pltpu.make_async_copy(gg, gg_out, out_sem.at[0])
     own.start()
     gv = jnp.sum(gacc[...], axis=0, keepdims=True)
     gsrc[0] = jnp.concatenate([gv[:, 128 * i : 128 * (i + 1)] for i in range(8)], axis=0)
     g0 = remote(gsrc.at[0], grecv.at[0], pair)
     g0.start()
-    merge(1, 2)
-    merge(1, 3)
-    x_second(1)
     g0.wait_recv()
     gsrc[1] = gsrc[0] + grecv[0]
     gain_send(1, dx)
+    a_done(0)
+    b_first(0)
+    a_done(1)
+    b_first(1)
     gain_sum(1)
     gain_send(2, dy)
-    x_done(0)
-    y_first(0)
+    b_second(0)
+    b_second(1)
     gain_sum(2)
     gain_send(3, dz)
-    y_second(0)
-    y_done(0)
+    b_done(0)
     z_first(0)
+    b_done(1)
+    z_first(1)
+    z_second(0)
+    z_second(1)
     gain_sum(3)
-    z_second(0)
-    x_done(1)
-    y_first(1)
     z_done(0)
-    y_second(1)
-    y_done(1)
-    z_first(1)
-    z_second(1)
     z_done(1)
 
     sub = lax.broadcasted_iota(jnp.int32, (8, 128), 0)
@@ -442,6 +491,12 @@
     for t in range(NCH):
         for cp in halo(t):
             cp.wait()
+    for t in range(N_RELAY):
+        land = relays(t)[2]
+
+        @pl.when((z == 0) | (z == 3))
+        def _():
+            land.wait_send()
     own.wait()
     g0.wait_send()
     for cp in started:
@@ -501,17 +556,17 @@
             pltpu.VMEM((FF, D), BF),
             pltpu.VMEM((512, D), BF),
             pltpu.VMEM((D, TOK), BF),
-            pltpu.VMEM((FF, TOK), BF),
+            pltpu.VMEM((8, 4, 64, TOK), BF),
             pltpu.VMEM((TOK, FF), BF),
             pltpu.VMEM((TOK, D), BF),
             pltpu.VMEM((512, D), F32),
             pltpu.VMEM((512, 128), F32),
             pltpu.VMEM((CH, D), F32),
-            pltpu.VMEM((2, 8, 16, 16, 1024), BF),
-            pltpu.VMEM((2, 4, 16, 16, 1024), BF),
-            pltpu.VMEM((2, 2, 8, 16, 1024), BF),
-            pltpu.VMEM((2, 2, 16, 16, 1024), BF),
-            pltpu.VMEM((2, 16, 16, 1024), BF),
+            pltpu.VMEM((2, 2, 4, 4, 4, 16, 1024), BF),
+            pltpu.VMEM((2, 4, 4, 4, 16, 1024), BF),
+            pltpu.VMEM((2, 2, 2, 4, 16, 1024), BF),
+            pltpu.VMEM((2, 2, 4, 4, 16, 1024), BF),
+            pltpu.VMEM((2, 4, 4, 16, 1024), BF),
             pltpu.VMEM((2, 2, 2, 16, 1024), BF),
             pltpu.VMEM((2, 2, 4, 16, 1024), BF),
             pltpu.VMEM((2, 4, 16, 1024), BF),
@@ -528,6 +583,9 @@
             pltpu.SemaphoreType.DMA((N_SEM,)),
             pltpu.SemaphoreType.DMA((2, NCH)),
             pltpu.SemaphoreType.DMA((2, NCH)),
+            pltpu.VMEM((N_RELAY, CH, D), BF),
+            pltpu.SemaphoreType.DMA((N_RELAY,)),
+            pltpu.SemaphoreType.DMA((N_RELAY,)),
         ],
         compiler_params=pltpu.CompilerParams(
             collective_id=0, has_side_effects=True, vmem_limit_bytes=60 * 1024 * 1024

time: 113 us -> 101 us (0.89)
  Pallas kernels: 110 us -> 97.8 us
    pallas_call x1, Pallas kernels: 99.4 us -> 87.3 us  [on_device(): pl.pallas_call(functools.partial(front, factor), name='front', out_shape=...]
where the time goes in v3:
time: 101 us; the launch traced here: 100 us
  Pallas kernels  97.8 us (97%)
  local copies, waits for them, and re-layouts  1.27 us (1%)
    pallas_call x1, Pallas kernels, on_device(): pl.pallas_call(functools.partial(front, factor), name='front', out_shape=...  87.3 us
    pallas_call x1, Pallas kernels, on_device(): pl.pallas_call(back, name='back', grid=(D // lanes,), out_shape=sds((48,...  10.5 us

profile of v3, /device:TPU:0, one launch (start us, length us, event | category | flops | bytes accessed | tf_op | source)
XLA Modules:
  0.0 100.3 jit_solution(5080700737268134422)
XLA Ops:
  0.6 87.3 %front.1 = (bf16[1024,1024]{1,0:T(8,128)(2,1)}, bf16[1024,1024]{1,0:T(8,128)(2,1)}, bf16[1024,1024]{1,0:T(8,128)(2,1)}, bf16[3,2,32,128]{3,2,1,0:T(8,128)(2,1)},...) custom-call(s32[1,3]{1,0:T(1,128)} %bitcast.11, bf16[1024,1024]{1,0:T(8,128)(2,1)} %bitcast.6, ...), custom_call_target="tpu_custom_call" | custom-call | tf_op jit(solution)/shard_map/front/pallas_call | solution.py:545
  88.0 0.0 copy-start.2
  88.0 0.0 copy-start.1
  88.0 0.0 copy-start
  88.0 10.5 %back.1 = bf16[48,48,1024]{2,1,0:T(8,128)(2,1)} custom-call(bf16[3,2,32,128]{3,2,1,0:T(8,128)(2,1)} %get-tuple-element.11.mats_ref, bf16[1024,1024]{1,0:T(8,128)(2,1)} %get-tuple-element.12.ga, bf16[1024,1024]{1,0:T(8,128)(2,1)} %get-tuple-element.13.gg, bf16[1024,1024]{1,0:T(8,128)(2,1)} %get-tuple-element.14.gb), custom_call_target="tpu_custom_call" | custom-call | tf_op jit(solution)/shard_map/back/pallas_call | solution.py:604
  98.4 0.0 copy-done.2
  98.4 0.6 reduce
  99.1 0.0 copy-done.1
  99.1 0.6 copy.14
  99.7 0.0 copy-done
  99.7 0.6 copy.15
Async XLA Ops:
  88.0 10.5 %copy-start.2 = (f32[8,1]{1,0:T(8,128)S(1)}, f32[8,1]{1,0:T(8,128)}, u32[]{:S(2)}) copy-start(f32[8,1]{1,0:T(8,128)} %get-tuple-element.17) | copy-start | bytes 100
  88.0 11.1 %copy-start.1 = (f32[8,2048]{1,0:T(8,128)S(1)}, f32[8,2048]{1,0:T(8,128)}, u32[]{:S(2)}) copy-start(f32[8,2048]{1,0:T(8,128)} %get-tuple-element.23) | copy-start | bytes 196612
  88.0 11.7 %copy-start = (f32[16,1024]{1,0:T(8,128)S(1)}, f32[16,1024]{1,0:T(8,128)}, u32[]{:S(2)}) copy-start(f32[16,1024]{1,0:T(8,128)} %get-tuple-element.24) | copy-start | bytes 196612

commit v4 on v3

--- a/solution.py
+++ b/solution.py
@@ -23,7 +23,7 @@
 NB = 1024
 LN = 512
 N_SEM = 64
-N_RELAY = 2
+RELAY = (2,)
 
 
 def nt(a, b):
@@ -152,7 +152,7 @@
         mats[k, 1, :, 0:48] = coli_ref[k]
     gacc[...] = jnp.zeros_like(gacc)
 
-    def forward(start, m):
+    def norm(start, m):
         gain = gain_ref[...]
         base = start % 512
 
@@ -169,6 +169,9 @@
             normed[r0 : r0 + CH, :] = nb
             normed_t[:, r1 : r1 + CH] = nb.T
 
+    def forward(start, m):
+        base = start % 512
+
         @pl.loop(0, FF // FB)
         def _(f):
             cols = pl.ds(pl.multiple_of(f * FB, FB), FB)
@@ -217,7 +220,7 @@
     def halo_start(t):
         src = gg.at[tokens(t)]
         to_lower, to_upper = halo(t)
-        if t >= N_RELAY:
+        if t not in RELAY:
             to_lower.start()
             to_upper.start()
             return
@@ -228,7 +231,7 @@
 
         @pl.when(z == 0)
         def _():
-            hop(src, relay.at[t], halo_send.at[0, t], relay_recv.at[t], dz(3)).start()
+            hop(src, relay.at[RELAY.index(t)], halo_send.at[0, t], relay_recv.at[RELAY.index(t)], dz(3)).start()
 
         @pl.when(z < 3)
         def _():
@@ -236,12 +239,34 @@
 
         @pl.when(z == 3)
         def _():
-            hop(src, relay.at[t], halo_send.at[1, t], relay_recv.at[t], dz(1)).start()
+            hop(src, relay.at[RELAY.index(t)], halo_send.at[1, t], relay_recv.at[RELAY.index(t)], dz(1)).start()
+
+    def halo_inner(t):
+        to_lower, to_upper = halo(t)
+
+        @pl.when(z > 0)
+        def _():
+            to_lower.start()
+
+        @pl.when(z < 3)
+        def _():
+            to_upper.start()
+
+    def halo_wrap(t):
+        to_lower, to_upper = halo(t)
+
+        @pl.when(z == 0)
+        def _():
+            to_lower.start()
+
+        @pl.when(z == 3)
+        def _():
+            to_upper.start()
 
     def relays(t):
-        down = hop(relay.at[t], ga_out.at[tokens(t)], relay_send.at[t], halo_recv.at[0, t], dy(3))
-        up = hop(relay.at[t], gb_out.at[tokens(t)], relay_send.at[t], halo_recv.at[1, t], dy(1))
-        land = hop(relay.at[t], relay.at[t], relay_send.at[t], relay_recv.at[t], dz(1))
+        down = hop(relay.at[RELAY.index(t)], ga_out.at[tokens(t)], relay_send.at[RELAY.index(t)], halo_recv.at[0, t], dy(3))
+        up = hop(relay.at[RELAY.index(t)], gb_out.at[tokens(t)], relay_send.at[RELAY.index(t)], halo_recv.at[1, t], dy(1))
+        land = hop(relay.at[RELAY.index(t)], relay.at[RELAY.index(t)], relay_send.at[RELAY.index(t)], relay_recv.at[RELAY.index(t)], dz(1))
         return down, up, land
 
     def relay_step(t):
@@ -257,7 +282,9 @@
             land.wait_recv()
             down.start()
 
-    for cp in loads[:4]:
+    loads[0].wait()
+    norm(0, CH)
+    for cp in loads[1:4]:
         cp.wait()
     forward(0, CH)
     backward(0)
@@ -269,9 +296,11 @@
     halo_start(0)
     for cp in loads[4:]:
         cp.wait()
+    norm(CH, CH)
     forward(CH, CH)
     backward(CH)
     halo_start(1)
+    norm(2 * CH, 2 * CH)
     forward(2 * CH, 2 * CH)
 
     at = ((x, y), (y, x))
@@ -427,7 +456,6 @@
     send_pair(1, 1)
     merge(1, 0)
     a_first(1)
-    relay_step(0)
     up_tiles(order[0][2], order[0][3])
     send_pair(0, 2)
     send_pair(0, 3)
@@ -444,16 +472,15 @@
     merge(0, 3)
     merge(1, 2)
     a_second(1)
-    relay_step(1)
     backward(3 * CH)
-    halo_start(3)
-    merge(1, 3)
+    halo_inner(3)
     own = pltpu.make_async_copy(gg, gg_out, out_sem.at[0])
     own.start()
     gv = jnp.sum(gacc[...], axis=0, keepdims=True)
     gsrc[0] = jnp.concatenate([gv[:, 128 * i : 128 * (i + 1)] for i in range(8)], axis=0)
     g0 = remote(gsrc.at[0], grecv.at[0], pair)
     g0.start()
+    merge(1, 3)
     g0.wait_recv()
     gsrc[1] = gsrc[0] + grecv[0]
     gain_send(1, dx)
@@ -465,6 +492,8 @@
     gain_send(2, dy)
     b_second(0)
     b_second(1)
+    relay_step(2)
+    halo_wrap(3)
     gain_sum(2)
     gain_send(3, dz)
     b_done(0)
@@ -491,7 +520,7 @@
     for t in range(NCH):
         for cp in halo(t):
             cp.wait()
-    for t in range(N_RELAY):
+    for t in RELAY:
         land = relays(t)[2]
 
         @pl.when((z == 0) | (z == 3))
@@ -583,9 +612,9 @@
             pltpu.SemaphoreType.DMA((N_SEM,)),
             pltpu.SemaphoreType.DMA((2, NCH)),
             pltpu.SemaphoreType.DMA((2, NCH)),
-            pltpu.VMEM((N_RELAY, CH, D), BF),
-            pltpu.SemaphoreType.DMA((N_RELAY,)),
-            pltpu.SemaphoreType.DMA((N_RELAY,)),
+            pltpu.VMEM((len(RELAY), CH, D), BF),
+            pltpu.SemaphoreType.DMA((len(RELAY),)),
+            pltpu.SemaphoreType.DMA((len(RELAY),)),
         ],
         compiler_params=pltpu.CompilerParams(
             collective_id=0, has_side_effects=True, vmem_limit_bytes=60 * 1024 * 1024

time: 101 us -> 91.5 us (0.906)
  Pallas kernels: 97.8 us -> 88.3 us
    pallas_call x1, Pallas kernels: 87.3 us -> 77.9 us  [on_device(): pl.pallas_call(functools.partial(front, factor), name='front', out_shape=...]
where the time goes in v4:
time: 91.5 us; the launch traced here: 90.9 us
  Pallas kernels  88.3 us (97%)
  local copies, waits for them, and re-layouts  1.27 us (1%)
    pallas_call x1, Pallas kernels, on_device(): pl.pallas_call(functools.partial(front, factor), name='front', out_shape=...  77.9 us
    pallas_call x1, Pallas kernels, on_device(): pl.pallas_call(back, name='back', grid=(D // lanes,), out_shape=sds((48,...  10.5 us

profile of v4, /device:TPU:0, one launch (start us, length us, event | category | flops | bytes accessed | tf_op | source)
XLA Modules:
  0.0 90.9 jit_solution(727199237821238538)
XLA Ops:
  0.6 77.9 %front.1 = (bf16[1024,1024]{1,0:T(8,128)(2,1)}, bf16[1024,1024]{1,0:T(8,128)(2,1)}, bf16[1024,1024]{1,0:T(8,128)(2,1)}, bf16[3,2,32,128]{3,2,1,0:T(8,128)(2,1)},...) custom-call(s32[1,3]{1,0:T(1,128)} %bitcast.11, bf16[1024,1024]{1,0:T(8,128)(2,1)} %bitcast.6, ...), custom_call_target="tpu_custom_call" | custom-call | tf_op jit(solution)/shard_map/front/pallas_call | solution.py:574
  78.5 0.0 copy-start.2
  78.5 0.0 copy-start.1
  78.6 0.0 copy-start
  78.6 10.5 %back.1 = bf16[48,48,1024]{2,1,0:T(8,128)(2,1)} custom-call(bf16[3,2,32,128]{3,2,1,0:T(8,128)(2,1)} %get-tuple-element.11.mats_ref, bf16[1024,1024]{1,0:T(8,128)(2,1)} %get-tuple-element.12.ga, bf16[1024,1024]{1,0:T(8,128)(2,1)} %get-tuple-element.13.gg, bf16[1024,1024]{1,0:T(8,128)(2,1)} %get-tuple-element.14.gb), custom_call_target="tpu_custom_call" | custom-call | tf_op jit(solution)/shard_map/back/pallas_call | solution.py:633
  89.0 0.0 copy-done.2
  89.0 0.6 reduce
  89.6 0.0 copy-done.1
  89.6 0.6 copy.14
  90.3 0.0 copy-done
  90.3 0.6 copy.15
Async XLA Ops:
  78.5 10.5 %copy-start.2 = (f32[8,1]{1,0:T(8,128)S(1)}, f32[8,1]{1,0:T(8,128)}, u32[]{:S(2)}) copy-start(f32[8,1]{1,0:T(8,128)} %get-tuple-element.17) | copy-start | bytes 100
  78.5 11.1 %copy-start.1 = (f32[8,2048]{1,0:T(8,128)S(1)}, f32[8,2048]{1,0:T(8,128)}, u32[]{:S(2)}) copy-start(f32[8,2048]{1,0:T(8,128)} %get-tuple-element.23) | copy-start | bytes 196612
  78.6 11.7 %copy-start = (f32[16,1024]{1,0:T(8,128)S(1)}, f32[16,1024]{1,0:T(8,128)}, u32[]{:S(2)}) copy-start(f32[16,1024]{1,0:T(8,128)} %get-tuple-element.24) | copy-start | bytes 196612

commit v5 on v4

--- a/solution.py
+++ b/solution.py
@@ -38,6 +38,26 @@
     return lax.dot_general(a, b, (((1,), (0,)), ((), ())), preferred_element_type=F32)
 
 
+def interp_blocks(b1, b2, mats):
+    r = lax.broadcasted_iota(jnp.int32, (384, 128), 0)
+    q = lax.broadcasted_iota(jnp.int32, (384, 128), 1)
+    pick_l = jnp.where(q == (r // 64) * 8 + r % 8, 1.0, 0.0).astype(BF)
+    pick_m = jnp.where(q == r // 8, 1.0, 0.0).astype(BF)
+    a = lax.broadcasted_iota(jnp.int32, (32, 256), 0)
+    b = lax.broadcasted_iota(jnp.int32, (32, 256), 1)
+    rep_j = jnp.where(b % 32 == a, 1.0, 0.0).astype(BF)
+    rep_i = jnp.where(b // 8 == a, 1.0, 0.0).astype(BF)
+    rr = lax.broadcasted_iota(jnp.int32, (384, 256), 0)
+    cc = lax.broadcasted_iota(jnp.int32, (384, 256), 1)
+    same_i = (rr // 8) % 8 == cc // 32
+    same_l = rr % 8 == cc % 8
+    for k in range(3):
+        col = nt(pick_l, mats[k][1]).astype(BF)
+        b1[k] = jnp.where(same_i, nn(col, rep_j), 0.0).astype(BF)
+        rw = nt(pick_m, mats[k][0]).astype(BF)
+        b2[:, k * 256 : (k + 1) * 256] = jnp.where(same_l, nn(rw, rep_i), 0.0).astype(BF)
+
+
 def front(
     factor,
     live_ref,
@@ -48,10 +68,8 @@
     gain_ref,
     rowi_ref,
     coli_ref,
-    gg_out,
-    ga_out,
-    gb_out,
-    mats_out,
+    half_out,
+    b2_out,
     up_out,
     down_out,
     gain_out,
@@ -91,6 +109,11 @@
     relay,
     relay_send,
     relay_recv,
+    ga,
+    gb,
+    b1,
+    hs,
+    hs_sem,
 ):
     zone = lax.axis_index("zone")
     row = lax.axis_index("row")
@@ -213,8 +236,8 @@
     def halo(t):
         src = gg.at[tokens(t)]
         return (
-            hop(src, ga_out.at[tokens(t)], halo_send.at[0, t], halo_recv.at[0, t], lower),
-            hop(src, gb_out.at[tokens(t)], halo_send.at[1, t], halo_recv.at[1, t], upper),
+            hop(src, ga.at[tokens(t)], halo_send.at[0, t], halo_recv.at[0, t], lower),
+            hop(src, gb.at[tokens(t)], halo_send.at[1, t], halo_recv.at[1, t], upper),
         )
 
     def halo_start(t):
@@ -264,8 +287,8 @@
             to_upper.start()
 
     def relays(t):
-        down = hop(relay.at[RELAY.index(t)], ga_out.at[tokens(t)], relay_send.at[RELAY.index(t)], halo_recv.at[0, t], dy(3))
-        up = hop(relay.at[RELAY.index(t)], gb_out.at[tokens(t)], relay_send.at[RELAY.index(t)], halo_recv.at[1, t], dy(1))
+        down = hop(relay.at[RELAY.index(t)], ga.at[tokens(t)], relay_send.at[RELAY.index(t)], halo_recv.at[0, t], dy(3))
+        up = hop(relay.at[RELAY.index(t)], gb.at[tokens(t)], relay_send.at[RELAY.index(t)], halo_recv.at[1, t], dy(1))
         land = hop(relay.at[RELAY.index(t)], relay.at[RELAY.index(t)], relay_send.at[RELAY.index(t)], relay_recv.at[RELAY.index(t)], dz(1))
         return down, up, land
 
@@ -430,6 +453,25 @@
             up_out[:, 1024:2048] = v[8:16]
         else:
             down_out[...] = v
+
+    half_copies = []
+
+    def columns(k, g):
+        slot = len(half_copies) % 4
+        if len(half_copies) >= 4:
+            half_copies[-4].wait()
+        src = (ga, gg, gb)[k]
+        h = nn(b1[k], src[g * CH : (g + 1) * CH, :]).astype(BF)
+        hs[slot] = h.reshape(6, 64, D)
+        cp = pltpu.make_async_copy(
+            hs.at[slot], half_out.at[:, pl.ds(k * 256 + g * 64, 64), :], hs_sem.at[slot])
+        cp.start()
+        half_copies.append(cp)
+
+    def received(t):
+        for k, cp in ((0, halo(t)[0]), (2, halo(t)[1])):
+            cp.wait_recv()
+            columns(k, t)
 
     gstage = {}
 
@@ -474,8 +516,11 @@
     a_second(1)
     backward(3 * CH)
     halo_inner(3)
-    own = pltpu.make_async_copy(gg, gg_out, out_sem.at[0])
-    own.start()
+    m_low.wait()
+    m_upp.wait()
+    interp_blocks(b1, b2_out, (mrecv.at[0], mats.at[1], mrecv.at[1]))
+    for g in range(NCH):
+        columns(1, g)
     gv = jnp.sum(gacc[...], axis=0, keepdims=True)
     gsrc[0] = jnp.concatenate([gv[:, 128 * i : 128 * (i + 1)] for i in range(8)], axis=0)
     g0 = remote(gsrc.at[0], grecv.at[0], pair)
@@ -488,12 +533,14 @@
     b_first(0)
     a_done(1)
     b_first(1)
+    received(0)
     gain_sum(1)
     gain_send(2, dy)
     b_second(0)
     b_second(1)
     relay_step(2)
     halo_wrap(3)
+    received(1)
     gain_sum(2)
     gain_send(3, dz)
     b_done(0)
@@ -502,6 +549,8 @@
     z_first(1)
     z_second(0)
     z_second(1)
+    received(2)
+    received(3)
     gain_sum(3)
     z_done(0)
     z_done(1)
@@ -512,52 +561,23 @@
     gain_out[...] = factor * jnp.sum(
         jnp.where(lane == 8 * row + sub, jnp.broadcast_to(line, (8, 128)), 0.0), axis=1, keepdims=True)
 
-    m_low.wait()
-    m_upp.wait()
-    mats_out[0] = mrecv[0]
-    mats_out[1] = mats[1]
-    mats_out[2] = mrecv[1]
     for t in range(NCH):
         for cp in halo(t):
-            cp.wait()
+            cp.wait_send()
+    for cp in half_copies[-4:]:
+        cp.wait()
     for t in RELAY:
         land = relays(t)[2]
 
         @pl.when((z == 0) | (z == 3))
         def _():
             land.wait_send()
-    own.wait()
     g0.wait_send()
     for cp in started:
         cp.wait_send()
 
 
-def back(mats_ref, ga, gg, gb, out, b1, b2, half):
-    @pl.when(pl.program_id(0) == 0)
-    def _():
-        r = lax.broadcasted_iota(jnp.int32, (384, 128), 0)
-        q = lax.broadcasted_iota(jnp.int32, (384, 128), 1)
-        pick_l = jnp.where(q == (r // 64) * 8 + r % 8, 1.0, 0.0).astype(BF)
-        pick_m = jnp.where(q == r // 8, 1.0, 0.0).astype(BF)
-        a = lax.broadcasted_iota(jnp.int32, (32, 256), 0)
-        b = lax.broadcasted_iota(jnp.int32, (32, 256), 1)
-        rep_j = jnp.where(b % 32 == a, 1.0, 0.0).astype(BF)
-        rep_i = jnp.where(b // 8 == a, 1.0, 0.0).astype(BF)
-        rr = lax.broadcasted_iota(jnp.int32, (384, 256), 0)
-        cc = lax.broadcasted_iota(jnp.int32, (384, 256), 1)
-        same_i = (rr // 8) % 8 == cc // 32
-        same_l = rr % 8 == cc % 8
-        for k in range(3):
-            col = nt(pick_l, mats_ref[k, 1]).astype(BF)
-            b1[k] = jnp.where(same_i, nn(col, rep_j), 0.0).astype(BF)
-            rw = nt(pick_m, mats_ref[k, 0]).astype(BF)
-            b2[:, k * 256 : (k + 1) * 256] = jnp.where(same_l, nn(rw, rep_i), 0.0).astype(BF)
-
-    for k, src in enumerate((ga, gg, gb)):
-        for g in range(4):
-            h = nn(b1[k], src[g * 256 : (g + 1) * 256, :]).astype(BF)
-            for lb in range(6):
-                half[lb, k * 256 + g * 64 : k * 256 + (g + 1) * 64, :] = h[lb * 64 : (lb + 1) * 64]
+def back(b2, half, out):
     for lp in range(3):
         a = nn(b2[...], half[2 * lp]).reshape(48, 8, -1)
         b = nn(b2[...], half[2 * lp + 1]).reshape(48, 8, -1)
@@ -570,14 +590,13 @@
     vmem = pl.BlockSpec(memory_space=pltpu.VMEM)
     smem = pl.BlockSpec(memory_space=pltpu.SMEM)
     sds = jax.ShapeDtypeStruct
-    grid_shape = sds((TOK, D), BF)
-    gg, ga, gb, mats, up, down, gain = pl.pallas_call(
+    half, b2, up, down, gain = pl.pallas_call(
         functools.partial(front, factor),
         name="front",
-        out_shape=(grid_shape, grid_shape, grid_shape, sds((3, 2, 32, 128), BF),
+        out_shape=(sds((6, 768, D), BF), sds((384, 768), BF),
                    sds((8, FF), F32), sds((16, D), F32), sds((8, 1), F32)),
         in_specs=[smem, hbm, hbm, hbm, hbm, vmem, vmem, vmem],
-        out_specs=(hbm, hbm, hbm, vmem, vmem, vmem, vmem),
+        out_specs=(hbm, vmem, vmem, vmem, vmem),
         scratch_shapes=[
             pltpu.VMEM((TOK, D), BF),
             pltpu.VMEM((TOK, D), BF),
@@ -615,9 +634,14 @@
             pltpu.VMEM((len(RELAY), CH, D), BF),
             pltpu.SemaphoreType.DMA((len(RELAY),)),
             pltpu.SemaphoreType.DMA((len(RELAY),)),
+            pltpu.VMEM((TOK, D), BF),
+            pltpu.VMEM((TOK, D), BF),
+            pltpu.VMEM((3, 384, 256), BF),
+            pltpu.VMEM((4, 6, 64, D), BF),
+            pltpu.SemaphoreType.DMA((4,)),
         ],
         compiler_params=pltpu.CompilerParams(
-            collective_id=0, has_side_effects=True, vmem_limit_bytes=60 * 1024 * 1024
+            collective_id=0, has_side_effects=True, vmem_limit_bytes=63 * 1024 * 1024
         ),
     )(
         pair_live[0],
@@ -635,16 +659,13 @@
         name="back",
         grid=(D // lanes,),
         out_shape=sds((48, 48, D), BF),
-        in_specs=[pl.BlockSpec((3, 2, 32, 128), lambda i: (0, 0, 0, 0))]
-        + [pl.BlockSpec((TOK, lanes), lambda i: (0, i))] * 3,
+        in_specs=[
+            pl.BlockSpec((384, 768), lambda i: (0, 0)),
+            pl.BlockSpec((6, 768, lanes), lambda i: (0, 0, i)),
+        ],
         out_specs=pl.BlockSpec((48, 48, lanes), lambda i: (0, 0, i)),
-        scratch_shapes=[
-            pltpu.VMEM((3, 384, 256), BF),
-            pltpu.VMEM((384, 768), BF),
-            pltpu.VMEM((6, 768, lanes), BF),
-        ],
         compiler_params=pltpu.CompilerParams(dimension_semantics=("arbitrary",)),
-    )(mats, ga, gg, gb)
+    )(b2, half)
     return source, up, down, gain.reshape(8)
 
 

time: 91.5 us -> 90.6 us (level)
    pallas_call x1, Pallas kernels: 10.5 us -> 8.41 us  [on_device(): pl.pallas_call(back, name='back', grid=(D // lanes,), out_shape=sds((48,...]
    pallas_call x1, Pallas kernels: 77.9 us -> 79 us  [on_device(): pl.pallas_call(functools.partial(front, factor), name='front', out_shape=...]
where the time goes in v5:
time: 90.6 us; the launch traced here: 90 us
  Pallas kernels  87.4 us (96%)
  local copies, waits for them, and re-layouts  1.27 us (1%)
    pallas_call x1, Pallas kernels, on_device(): pl.pallas_call(functools.partial(front, factor), name='front', out_shape=...  79 us
    pallas_call x1, Pallas kernels, on_device(): pl.pallas_call(back, name='back', grid=(D // lanes,), out_shape=sds((48,...  8.41 us

profile of v5, /device:TPU:0, one launch (start us, length us, event | category | flops | bytes accessed | tf_op | source)
XLA Modules:
  0.0 90.0 jit_solution(1844616727037116593)
XLA Ops:
  0.6 79.0 %front.1 = (bf16[6,768,1024]{2,1,0:T(8,128)(2,1)}, bf16[384,768]{1,0:T(8,128)(2,1)}, f32[8,2048]{1,0:T(8,128)}, f32[16,1024]{1,0:T(8,128)}, f32[8,1]{1,0:T(8,128)}) custom-call(s32[1,3]{1,0:T(1,128)} %bitcast.11, bf16[1024,1024]{1,0:T(8,128)(2,1)} %bitcast.6, bf16[1024,1024]{1,0:T(8,128)(2,1)} %bitcast.7, bf16[1024,2048]{1,0:T(8,128)(2,1)} %wu_hbm.1, ...), custom_call_target="tpu_custom_call" | custom-call | tf_op jit(solution)/shard_map/front/pallas_call | solution.py:593
  79.6 0.0 copy-start.2
  79.6 0.0 copy-start.1
  79.7 0.0 copy-start
  79.7 8.4 %back.1 = bf16[48,48,1024]{2,1,0:T(8,128)(2,1)} custom-call(bf16[384,768]{1,0:T(8,128)(2,1)} %get-tuple-element.9.b2, bf16[6,768,1024]{2,1,0:T(8,128)(2,1)} %get-tuple-element.10.half), custom_call_target="tpu_custom_call" | custom-call | tf_op jit(solution)/shard_map/back/pallas_call | solution.py:657
  88.1 0.0 copy-done.2
  88.1 0.6 reduce
  88.7 0.0 copy-done.1
  88.7 0.6 copy.14
  89.3 0.0 copy-done
  89.3 0.6 copy.15
Async XLA Ops:
  79.6 8.4 %copy-start.2 = (f32[8,1]{1,0:T(8,128)S(1)}, f32[8,1]{1,0:T(8,128)}, u32[]{:S(2)}) copy-start(f32[8,1]{1,0:T(8,128)} %get-tuple-element.13) | copy-start | bytes 100
  79.6 9.1 %copy-start.1 = (f32[8,2048]{1,0:T(8,128)S(1)}, f32[8,2048]{1,0:T(8,128)}, u32[]{:S(2)}) copy-start(f32[8,2048]{1,0:T(8,128)} %get-tuple-element.19) | copy-start | bytes 196612
  79.7 9.7 %copy-start = (f32[16,1024]{1,0:T(8,128)S(1)}, f32[16,1024]{1,0:T(8,128)}, u32[]{:S(2)}) copy-start(f32[16,1024]{1,0:T(8,128)} %get-tuple-element.20) | copy-start | bytes 196612
